TPU v7x, 32 devices: a whole 2x2x4 slice. The times are simulated.
32 devices in a mesh: dp: 4 (over y, x), fsdp: 8 (over z, core).
Axes of the slice: x: 2, y: 2, z: 4, core: 2. Of those that a mesh axis runs over, the one named last changes fastest.
Arguments:
- latents: float32 [128, 128, 384], P(('dp', 'fsdp')), may hold values from -6 to 6
- conditioning: float32 [128, 384], P(('dp', 'fsdp')), may hold values from -6 to 6
- counts: int32 [32], P(('dp', 'fsdp')), may hold values from 1 to 4, as said below
- cotangent: float32 [128, 128, 384], P(('dp', 'fsdp')), may hold values from -6 to 6
- ada_weights: bfloat16 [884736], P(('dp', 'fsdp')), may hold values from -0.3125 to 0.3125
- attn_weights: bfloat16 [589824], P(('dp', 'fsdp'))
- mlp_weights: bfloat16 [1179648], P(('dp', 'fsdp'))
- flat_biases: bfloat16 [5376], P(('dp', 'fsdp')), may hold values from -3 to 3
Outputs:
- output: float32 [128, 128, 384], P(('dp', 'fsdp'))
- grad_latents: float32 [128, 128, 384], P(('dp', 'fsdp'))
- grad_conditioning: float32 [128, 384], P(('dp', 'fsdp'))
- grad_ada_weights: float32 [884736], P(('dp', 'fsdp'))
- grad_attn_weights: float32 [589824], P(('dp', 'fsdp'))
- grad_mlp_weights: float32 [1179648], P(('dp', 'fsdp'))
- grad_biases: float32 [5376], P(('dp', 'fsdp'))
Inputs may be any that keep to these rules, and one draw needn't show every extreme that they name: `counts`: slots of a device at or beyond its count hold padding; in every draw some device holds 4 live latents and some holds 1.
All inputs are finite; a program needn't handle non-finite values.
Results may differ from a plain program's by a relative error of at most 0.0095.
The roundings to bfloat16 on the way count: a program that leaves them out, or rounds other values in their place, can miss the bound.
Values may be sent and summed in bfloat16 or wider, within the bound.
A program may use at most 128 MiB of HBM per device.

v0:
```python
from functools import partial

import jax
import jax.numpy as jnp
from jax import lax
from jax.sharding import PartitionSpec as P

FF = 1536
HEADS = 6


EPSILON = 1e-06
GELU_COEF = 0.044715
ROOT_TWO_OVER_PI = 0.7978845608028654


def layer_norm(values):
    centre = values - jnp.mean(values, axis=-1, keepdims=True)
    inverse = lax.rsqrt(jnp.mean(centre * centre, axis=-1, keepdims=True) + EPSILON)
    return (centre * inverse, inverse)


def norm_backward(grad_norm, normed, inverse):
    first = jnp.mean(grad_norm, axis=-1, keepdims=True)
    second = jnp.mean(grad_norm * normed, axis=-1, keepdims=True)
    return (grad_norm - first - normed * second) * inverse


def gelu_value(pre_act):
    inner = ROOT_TWO_OVER_PI * (pre_act + GELU_COEF * pre_act * pre_act * pre_act)
    return 0.5 * pre_act * (1.0 + jnp.tanh(inner))


def gelu_slope(pre_act):
    tanh_part = jnp.tanh(ROOT_TWO_OVER_PI * (pre_act + GELU_COEF * pre_act * pre_act * pre_act))
    return 0.5 * (1.0 + tanh_part) + 0.5 * pre_act * (
        1.0 - tanh_part * tanh_part
    ) * ROOT_TWO_OVER_PI * (1.0 + 3.0 * GELU_COEF * pre_act * pre_act)


def silu_slope(values):
    sigma = jax.nn.sigmoid(values)
    return sigma * (1.0 + values * (1.0 - sigma))


def product(form, left, right):
    return jnp.einsum(form, left, right, preferred_element_type=jnp.float32)


def mat_dot(left, right):
    return jnp.dot(left, right, preferred_element_type=jnp.float32)


def unpack(ada_flat, attn_flat, mlp_flat, bias_flat, model_width, hidden_units):
    qkv_size = 3 * model_width * model_width
    fc1_size = model_width * hidden_units
    pieces = [
        ada_flat.reshape(model_width, 6 * model_width),
        attn_flat[:qkv_size].reshape(model_width, 3 * model_width),
        attn_flat[qkv_size:].reshape(model_width, model_width),
        mlp_flat[:fc1_size].reshape(model_width, hidden_units),
        mlp_flat[fc1_size:].reshape(hidden_units, model_width),
    ]
    offset = 0
    for extent_now in [
        6 * model_width,
        model_width,
        model_width,
        model_width,
        hidden_units,
        model_width,
    ]:
        pieces.append(bias_flat[offset : offset + extent_now])
        offset = offset + extent_now
    return tuple(pieces)


def forward_group(latent_rows, cond_rows, live_rows, weights, head_count):
    w_ada, w_qkv, w_proj, w_fc1, w_fc2, b_ada, b_query, b_value, b_proj, b_fc1, b_fc2 = weights
    groups, length, model_width = latent_rows.shape
    head_dim = model_width // head_count
    row_count = groups * length
    score_scale = head_dim ** (-0.5)
    cond_act = jax.nn.silu(cond_rows).astype(jnp.bfloat16)
    modulation = mat_dot(cond_act, w_ada) + b_ada.astype(jnp.float32)
    parts = [modulation[:, None, k * model_width : (k + 1) * model_width] for k in range(6)]
    shift_attn, scale_attn, gate_attn, shift_mlp, scale_mlp, gate_mlp = parts
    norm_one, inverse_one = layer_norm(latent_rows)
    modulated_one = (norm_one * (1.0 + scale_attn) + shift_attn).astype(jnp.bfloat16)
    projected = mat_dot(modulated_one.reshape(row_count, model_width), w_qkv)
    query_rows = (
        (projected[:, :model_width] + b_query.astype(jnp.float32))
        .astype(jnp.bfloat16)
        .reshape(groups, length, model_width)
    )
    key_rows = (
        projected[:, model_width : 2 * model_width]
        .astype(jnp.bfloat16)
        .reshape(groups, length, model_width)
    )
    value_rows = (
        (projected[:, 2 * model_width :] + b_value.astype(jnp.float32))
        .astype(jnp.bfloat16)
        .reshape(groups, length, model_width)
    )
    split_shape = (groups, length, head_count, head_dim)
    scores = (
        product("gqhe,gkhe->ghqk", query_rows.reshape(split_shape), key_rows.reshape(split_shape))
        * score_scale
    )
    log_total = jnp.log(jnp.sum(jnp.exp(scores), axis=-1, keepdims=True))
    probs = jnp.exp(scores - log_total).astype(jnp.bfloat16)
    mixed = (
        product("ghqk,gkhe->gqhe", probs, value_rows.reshape(split_shape))
        .astype(jnp.bfloat16)
        .reshape(row_count, model_width)
    )
    branch = (mat_dot(mixed, w_proj) + b_proj.astype(jnp.float32)).reshape(
        groups, length, model_width
    )
    after_attn = latent_rows + gate_attn * branch
    norm_two, inverse_two = layer_norm(after_attn)
    modulated_two = (norm_two * (1.0 + scale_mlp) + shift_mlp).astype(jnp.bfloat16)
    pre_act = mat_dot(modulated_two.reshape(row_count, model_width), w_fc1) + b_fc1.astype(
        jnp.float32
    )
    activated = gelu_value(pre_act).astype(jnp.bfloat16)
    mlp_rows = (mat_dot(activated, w_fc2) + b_fc2.astype(jnp.float32)).reshape(
        groups, length, model_width
    )
    output = jnp.where(live_rows[:, None, None], after_attn + gate_mlp * mlp_rows, 0.0)
    hidden_units = pre_act.shape[1]
    saved = (
        cond_act,
        modulation,
        norm_one,
        inverse_one,
        modulated_one,
        query_rows,
        key_rows,
        value_rows,
        log_total[..., 0],
        mixed.reshape(groups, length, model_width),
        branch,
        norm_two,
        inverse_two,
        modulated_two,
        pre_act.reshape(groups, length, hidden_units),
        activated.reshape(groups, length, hidden_units),
        mlp_rows,
    )
    return (output, saved)


def mlp_backward(saved, cotangent_rows, live_rows, weights):
    w_fc1 = weights[3]
    w_fc2 = weights[4]
    (
        cond_act,
        modulation,
        norm_one,
        inverse_one,
        modulated_one,
        query_rows,
        key_rows,
        value_rows,
        log_total,
        mixed,
        branch,
        norm_two,
        inverse_two,
        modulated_two,
        pre_act,
        activated,
        mlp_rows,
    ) = saved
    groups, length, model_width = cotangent_rows.shape
    hidden_units = pre_act.shape[2]
    row_count = groups * length
    scale_mlp = modulation[:, None, 4 * model_width : 5 * model_width]
    gate_mlp = modulation[:, None, 5 * model_width : 6 * model_width]
    grad_out = jnp.where(live_rows[:, None, None], cotangent_rows, 0.0)
    grad_gate_mlp = jnp.sum(grad_out * mlp_rows, axis=1)
    grad_mlp_full = grad_out * gate_mlp
    bias_fc2 = jnp.sum(grad_mlp_full, axis=(0, 1))
    grad_mlp = grad_mlp_full.astype(jnp.bfloat16).reshape(row_count, model_width)
    weight_fc2 = mat_dot(activated.reshape(row_count, hidden_units).T, grad_mlp)
    grad_pre_full = mat_dot(grad_mlp, w_fc2.T) * gelu_slope(
        pre_act.reshape(row_count, hidden_units)
    )
    bias_fc1 = jnp.sum(grad_pre_full, axis=0)
    grad_pre = grad_pre_full.astype(jnp.bfloat16)
    weight_fc1 = mat_dot(modulated_two.reshape(row_count, model_width).T, grad_pre)
    grad_two = mat_dot(grad_pre, w_fc1.T).reshape(groups, length, model_width)
    grad_scale_mlp = jnp.sum(grad_two * norm_two, axis=1)
    grad_shift_mlp = jnp.sum(grad_two, axis=1)
    grad_after = grad_out + norm_backward(grad_two * (1.0 + scale_mlp), norm_two, inverse_two)
    mod_tail = jnp.concatenate([grad_shift_mlp, grad_scale_mlp, grad_gate_mlp], axis=1)
    return (grad_after, mod_tail, (weight_fc1, weight_fc2, bias_fc1, bias_fc2))


def attention_backward(saved, cond_rows, grad_after, mod_tail, weights, head_count):
    w_ada = weights[0]
    w_qkv = weights[1]
    w_proj = weights[2]
    (
        cond_act,
        modulation,
        norm_one,
        inverse_one,
        modulated_one,
        query_rows,
        key_rows,
        value_rows,
        log_total,
        mixed,
        branch,
        norm_two,
        inverse_two,
        modulated_two,
        pre_act,
        activated,
        mlp_rows,
    ) = saved
    groups, length, model_width = grad_after.shape
    head_dim = model_width // head_count
    row_count = groups * length
    score_scale = head_dim ** (-0.5)
    scale_attn = modulation[:, None, model_width : 2 * model_width]
    gate_attn = modulation[:, None, 2 * model_width : 3 * model_width]
    grad_gate_attn = jnp.sum(grad_after * branch, axis=1)
    grad_branch_full = grad_after * gate_attn
    bias_proj = jnp.sum(grad_branch_full, axis=(0, 1))
    grad_branch = grad_branch_full.astype(jnp.bfloat16).reshape(row_count, model_width)
    weight_proj = mat_dot(mixed.reshape(row_count, model_width).T, grad_branch)
    grad_mixed = mat_dot(grad_branch, w_proj.T).astype(jnp.bfloat16)
    split_shape = (groups, length, head_count, head_dim)
    query_split = query_rows.reshape(split_shape)
    key_split = key_rows.reshape(split_shape)
    value_split = value_rows.reshape(split_shape)
    mixed_split = grad_mixed.reshape(split_shape)
    scores = product("gqhe,gkhe->ghqk", query_split, key_split) * score_scale
    probs_full = jnp.exp(scores - log_total[..., None])
    grad_probs = product("gqhe,gkhe->ghqk", mixed_split, value_split)
    grad_value = product("ghqk,gqhe->gkhe", probs_full.astype(jnp.bfloat16), mixed_split).astype(
        jnp.bfloat16
    )
    delta_rows = jnp.sum(probs_full * grad_probs, axis=-1, keepdims=True)
    grad_scores = (probs_full * (grad_probs - delta_rows) * score_scale).astype(jnp.bfloat16)
    grad_query = product("ghqk,gkhe->gqhe", grad_scores, key_split).astype(jnp.bfloat16)
    grad_key = product("ghqk,gqhe->gkhe", grad_scores, query_split).astype(jnp.bfloat16)
    grad_query = grad_query.reshape(row_count, model_width)
    grad_key = grad_key.reshape(row_count, model_width)
    grad_value = grad_value.reshape(row_count, model_width)
    grad_proj_in = jnp.concatenate([grad_query, grad_key, grad_value], axis=1)
    weight_qkv = mat_dot(modulated_one.reshape(row_count, model_width).T, grad_proj_in)
    bias_query = jnp.sum(grad_query.astype(jnp.float32), axis=0)
    bias_value = jnp.sum(grad_value.astype(jnp.float32), axis=0)
    grad_one = mat_dot(grad_proj_in, w_qkv.T).reshape(groups, length, model_width)
    grad_scale_attn = jnp.sum(grad_one * norm_one, axis=1)
    grad_shift_attn = jnp.sum(grad_one, axis=1)
    grad_input = grad_after + norm_backward(grad_one * (1.0 + scale_attn), norm_one, inverse_one)
    grad_mod_full = jnp.concatenate(
        [grad_shift_attn, grad_scale_attn, grad_gate_attn, mod_tail], axis=1
    )
    bias_ada = jnp.sum(grad_mod_full, axis=0)
    grad_mod = grad_mod_full.astype(jnp.bfloat16)
    weight_ada = mat_dot(cond_act.T, grad_mod)
    grad_cond = mat_dot(grad_mod, w_ada.T) * silu_slope(cond_rows)
    return (
        grad_input,
        grad_cond,
        (weight_ada, weight_qkv, weight_proj, bias_ada, bias_query, bias_value, bias_proj),
    )


def empty_saved(slot_count, length, model_width, hidden_units, head_count):
    plain = (slot_count, length, model_width)
    wide = (slot_count, length, hidden_units)
    column = (slot_count, length, 1)
    return (
        jnp.zeros((slot_count, model_width), jnp.bfloat16),
        jnp.zeros((slot_count, 6 * model_width), jnp.float32),
        jnp.zeros(plain, jnp.float32),
        jnp.zeros(column, jnp.float32),
        jnp.zeros(plain, jnp.bfloat16),
        jnp.zeros(plain, jnp.bfloat16),
        jnp.zeros(plain, jnp.bfloat16),
        jnp.zeros(plain, jnp.bfloat16),
        jnp.zeros((slot_count, head_count, length), jnp.float32),
        jnp.zeros(plain, jnp.bfloat16),
        jnp.zeros(plain, jnp.float32),
        jnp.zeros(plain, jnp.float32),
        jnp.zeros(column, jnp.float32),
        jnp.zeros(plain, jnp.bfloat16),
        jnp.zeros(wide, jnp.float32),
        jnp.zeros(wide, jnp.bfloat16),
        jnp.zeros(plain, jnp.float32),
    )


def take_rows(buffer, start, group_width):
    return lax.dynamic_slice_in_dim(buffer, start, group_width, 0)


def place_rows(buffer, piece, start):
    return lax.dynamic_update_slice_in_dim(buffer, piece, start, 0)


def zeros_for(weights, picks):
    return tuple((jnp.zeros(weights[k].shape, jnp.float32) for k in picks))


def add_terms(totals, terms):
    return tuple((total + term for total, term in zip(totals, terms)))


def local(
    latents, conditioning, counts, cotangent, ada_weights, attn_weights, mlp_weights, flat_biases
):
    slot_count, length, model_width = latents.shape
    group_width = 2
    mlp_picks = (3, 4, 9, 10)
    attn_picks = (0, 1, 2, 5, 6, 7, 8)
    gathered = (
        lax.all_gather(ada_weights, ("dp", "fsdp"), axis=0, tiled=True),
        lax.all_gather(attn_weights, ("dp", "fsdp"), axis=0, tiled=True),
        lax.all_gather(mlp_weights, ("dp", "fsdp"), axis=0, tiled=True),
        lax.all_gather(flat_biases, ("dp", "fsdp"), axis=0, tiled=True),
    )
    weights = unpack(gathered[0], gathered[1], gathered[2], gathered[3], model_width, FF)
    own_count = counts[0]
    live = jnp.arange(slot_count, dtype=jnp.int32) < own_count
    turns = slot_count // group_width

    def forward_step(turn, carry):
        out_buffer, saved_buffer = carry
        start = turn * group_width
        output, saved = forward_group(
            take_rows(latents, start, group_width),
            take_rows(conditioning, start, group_width),
            take_rows(live, start, group_width),
            weights,
            HEADS,
        )
        saved_buffer = jax.tree.map(partial(place_rows, start=start), saved_buffer, saved)
        return (place_rows(out_buffer, output, start), saved_buffer)

    start_state = (
        jnp.zeros(latents.shape, jnp.float32),
        empty_saved(slot_count, length, model_width, FF, HEADS),
    )
    out_buffer, saved_buffer = lax.fori_loop(0, turns, forward_step, start_state)
    again = (
        lax.all_gather(ada_weights, ("dp", "fsdp"), axis=0, tiled=True),
        lax.all_gather(attn_weights, ("dp", "fsdp"), axis=0, tiled=True),
        lax.all_gather(mlp_weights, ("dp", "fsdp"), axis=0, tiled=True),
        lax.all_gather(flat_biases, ("dp", "fsdp"), axis=0, tiled=True),
    )
    back_weights = unpack(again[0], again[1], again[2], again[3], model_width, FF)

    def saved_rows(start):
        return jax.tree.map(partial(take_rows, start=start, group_width=group_width), saved_buffer)

    def both_step(turn, carry):
        grad_buffer, cond_buffer, attn_totals, mlp_totals = carry
        start = turn * group_width
        saved_piece = saved_rows(start)
        grad_after, mod_tail, mlp_terms = mlp_backward(
            saved_piece,
            take_rows(cotangent, start, group_width),
            take_rows(live, start, group_width),
            back_weights,
        )
        grad_input, grad_cond, attn_terms = attention_backward(
            saved_piece,
            take_rows(conditioning, start, group_width),
            grad_after,
            mod_tail,
            back_weights,
            HEADS,
        )
        return (
            place_rows(grad_buffer, grad_input, start),
            place_rows(cond_buffer, grad_cond, start),
            add_terms(attn_totals, attn_terms),
            add_terms(mlp_totals, mlp_terms),
        )

    both_state = (
        jnp.zeros(latents.shape, jnp.float32),
        jnp.zeros(conditioning.shape, jnp.float32),
        zeros_for(back_weights, attn_picks),
        zeros_for(back_weights, mlp_picks),
    )
    grad_latents, grad_conditioning, attn_totals, mlp_totals = lax.fori_loop(
        0, turns, both_step, both_state
    )
    ada_terms = attn_totals[0].reshape(-1)
    attn_flat_terms = jnp.concatenate([attn_totals[1].reshape(-1), attn_totals[2].reshape(-1)])
    mlp_flat_terms = jnp.concatenate([mlp_totals[0].reshape(-1), mlp_totals[1].reshape(-1)])
    bias_terms = jnp.concatenate(
        [
            attn_totals[3],
            attn_totals[4],
            attn_totals[5],
            attn_totals[6],
            mlp_totals[2],
            mlp_totals[3],
        ]
    )
    grad_ada, grad_attn, grad_mlp, grad_biases = (
        lax.psum_scatter(ada_terms, ("dp", "fsdp"), scatter_dimension=0, tiled=True),
        lax.psum_scatter(attn_flat_terms, ("dp", "fsdp"), scatter_dimension=0, tiled=True),
        lax.psum_scatter(mlp_flat_terms, ("dp", "fsdp"), scatter_dimension=0, tiled=True),
        lax.psum_scatter(bias_terms, ("dp", "fsdp"), scatter_dimension=0, tiled=True),
    )
    return (out_buffer, grad_latents, grad_conditioning, grad_ada, grad_attn, grad_mlp, grad_biases)


def solution(mesh):
    in_specs = (
        P(("dp", "fsdp"), None, None),
        P(("dp", "fsdp"), None),
        P(("dp", "fsdp")),
        P(("dp", "fsdp"), None, None),
        P(("dp", "fsdp")),
        P(("dp", "fsdp")),
        P(("dp", "fsdp")),
        P(("dp", "fsdp")),
    )
    out_specs = (
        P(("dp", "fsdp"), None, None),
        P(("dp", "fsdp"), None, None),
        P(("dp", "fsdp"), None),
        P(("dp", "fsdp")),
        P(("dp", "fsdp")),
        P(("dp", "fsdp")),
        P(("dp", "fsdp")),
    )
    return jax.shard_map(local, mesh=mesh, in_specs=in_specs, out_specs=out_specs, check_vma=False)
```

profile of v0, /device:TPU:0, one launch (start us, length us, event | category | flops | bytes accessed | tf_op | source)
XLA Modules:
  0.0 619.1 jit_solution(107145477465439296)
XLA Ops:
  10.3 42.1 %all-reduce = bf16[5376]{0:T(1024)(128)(2,1)S(1)} all-reduce(bf16[5376]{0:T(1024)(128)(2,1)S(1)} %dynamic-update-slice), channel_id=1, replica_groups=mesh['dp'=4,'fsdp'=8] {'dp','fsdp'}, use_global_device_ids=true, to_apply=%add | all-reduce | flops 5376 | bytes 21504
  54.4 13.5 %all-gather.6.cloned.1.call-done = bf16[589824]{0:T(1024)(128)(2,1)} async-done(((bf16[18432]{0:T(1024)(128)(2,1)}), bf16[589824]{0:T(1024)(128)(2,1)}) %all-gather.6.cloned.1.call-update) | async-done | bytes 1179664 | tf_op jit(solution)/shard_map/all_gather | solution.py:327
  71.9 53.4 %all-gather.4.cloned.1.call-done = bf16[884736]{0:T(1024)(128)(2,1)} async-done(((bf16[27648]{0:T(1024)(128)(2,1)}), bf16[884736]{0:T(1024)(128)(2,1)}) %all-gather.4.cloned.1.call-update) | async-done | bytes 1769488 | tf_op jit(solution)/shard_map/all_gather | solution.py:326
  125.2 3.6 reshape.435
  128.8 55.6 %all-gather.8.cloned.1.call-done = bf16[1179648]{0:T(1024)(128)(2,1)} async-done(((bf16[36864]{0:T(1024)(128)(2,1)}), bf16[1179648]{0:T(1024)(128)(2,1)}) %all-gather.8.cloned.1.call-update) | async-done | bytes 2359312 | tf_op jit(solution)/shard_map/all_gather | solution.py:328
  184.4 2.8 fusion.69
  189.4 2.3 slice.178
  206.8 58.9 %while.85 = (s32[]{:T(128)}, f32[4,128,384]{2,1,0:T(8,128)}, bf16[4,384]{1,0:T(4,128)(2,1)}, f32[4,2304]{1,0:T(4,128)}, f32[4,128,384]{2,1,0:T(8,128)}, /*index=...) while((s32[]{:T(128)}, f32[4,128,384]{2,1,0:T(8,128)}, ...), condition=%wide.region_6.7_spmd, body=%wide.region_0.6_spmd.sunk | while | flops 967920384 | bytes 133319112 | solution.py:353
  217.3 2.2 exponential_reduce_fusion.2
  246.7 2.2 exponential_reduce_fusion.2
  267.3 105.5 %while.86 = (s32[]{:T(128)}, f32[4,128,384]{2,1,0:T(8,128)}, f32[4,384]{1,0:T(4,128)}, f32[384,2304]{1,0:T(8,128)}, f32[384,1152]{1,0:T(8,128)}, /*index=5*/f32[...) while((s32[]{:T(128)}, f32[4,128,384]{2,1,0:T(8,128)}, ...), condition=%wide.region_25.26_spmd.clone, body=%wide.region_7.25_spmd.clone.sunk | while | flops 1965417472 | bytes 160682800 | solution.py:396
  292.4 3.0 convert_reduce_fusion.4
  295.7 3.0 fusion.206
  305.4 2.4 convolution_add_fusion.14
  343.2 3.0 convert_reduce_fusion.4
  346.4 3.0 fusion.206
  356.1 4.6 convolution_add_fusion.14
  366.4 3.8 convolution_add_fusion.16
  372.8 4.7 reshape.436
  380.0 3.4 reshape.440
  385.0 3.2 pad_maximum_fusion.1
  388.2 4.2 pad_maximum_fusion
  393.3 39.6 %all-reduce.4 = f32[5376]{0:T(1024)S(1)} all-reduce(f32[5376]{0:T(1024)S(1)} %constant_dynamic-update-slice_fusion.21), channel_id=5, replica_groups=mesh['dp'=4,'fsdp'=8] {'dp','fsdp'}, use_global_device_ids=true, to_apply=%region_29.30.clone | all-reduce | flops 5376 | bytes 43008
  433.5 174.4 %all-reduce.8.cloned.1.call-done = (f32[884736]{0:T(1024)}, f32[589824]{0:T(1024)}, f32[1179648]{0:T(1024)}) async-done(((f32[884736]{0:T(1024)}, f32[589824]{0:T(1024)}, f32[1179648]{0:T(1024)}), (f32[884736]{0:T(1024)}, f32[589824]{0:T(1024)}, f32[1179648]{0:T(1024)})) %all-reduce.8.cloned.1.call-update) | async-done | bytes 10616848
  (720 shorter events, 171.4 us)
Async XLA Ops:
  7.2 60.7 %all-gather.6.cloned.1.call-start = ((), (), s32[]{:S(2)}) async-start(), calls=%async_computation.1 | async-start | bytes 1216512 | tf_op jit(solution)/shard_map/all_gather | solution.py:327
  7.9 117.3 %all-gather.4.cloned.1.call-start = ((), (), s32[]{:S(2)}) async-start(), calls=%async_computation | async-start | bytes 1824768 | tf_op jit(solution)/shard_map/all_gather | solution.py:326
  8.6 175.8 %all-gather.8.cloned.1.call-start = ((), (), s32[]{:S(2)}) async-start(), calls=%async_computation.2 | async-start | bytes 2433024 | tf_op jit(solution)/shard_map/all_gather | solution.py:328
  9.4 598.5 %all-reduce.8.cloned.1.call-start = ((), (), s32[]{:S(2)}) async-start(), calls=%async_computation.3 | async-start | bytes 21233664
  52.4 18.5 %copy-start.80 = (bf16[5376]{0:T(1024)(128)(2,1)}, bf16[5376]{0:T(1024)(128)(2,1)S(1)}, u32[]{:S(2)}) copy-start(bf16[5376]{0:T(1024)(128)(2,1)S(1)} %all-reduce) | copy-start | bytes 32260
  206.8 6.7 %copy-start.109 = (bf16[384]{0:T(512)(128)(2,1)}, bf16[384]{0:T(512)(128)(2,1)S(1)}, u32[]{:S(2)}) copy-start(bf16[384]{0:T(512)(128)(2,1)S(1)} %get-tuple-element.2479) | copy-start | bytes 2308 | tf_op jit(solution)/shard_map/while
  206.8 6.7 %copy-start.107 = (bf16[384]{0:T(512)(128)(2,1)}, bf16[384]{0:T(512)(128)(2,1)S(1)}, u32[]{:S(2)}) copy-start(bf16[384]{0:T(512)(128)(2,1)S(1)} %get-tuple-element.2480) | copy-start | bytes 2308 | tf_op jit(solution)/shard_map/while
  236.3 6.8 %copy-start.109 = (bf16[384]{0:T(512)(128)(2,1)}, bf16[384]{0:T(512)(128)(2,1)S(1)}, u32[]{:S(2)}) copy-start(bf16[384]{0:T(512)(128)(2,1)S(1)} %get-tuple-element.2479) | copy-start | bytes 2308 | tf_op jit(solution)/shard_map/while
  236.3 6.7 %copy-start.107 = (bf16[384]{0:T(512)(128)(2,1)}, bf16[384]{0:T(512)(128)(2,1)S(1)}, u32[]{:S(2)}) copy-start(bf16[384]{0:T(512)(128)(2,1)S(1)} %get-tuple-element.2480) | copy-start | bytes 2308 | tf_op jit(solution)/shard_map/while
  267.3 7.4 %copy-start.46 = (bf16[4,128,384]{2,1,0:T(8,128)(2,1)}, bf16[4,128,384]{2,1,0:T(8,128)(2,1)S(1)}, u32[]{:S(2)}) copy-start(bf16[4,128,384]{2,1,0:T(8,128)(2,1)S(1)} %get-tuple-element.2622) | copy-start | bytes 1179652 | tf_op jit(solution)/shard_map/while
  276.6 5.2 copy-start.86
  278.8 7.6 %copy-start.23 = (bf16[384,384]{1,0:T(8,128)(2,1)S(1)}, bf16[384,384]{1,0:T(8,128)(2,1)}, u32[]{:S(2)}) copy-start(bf16[384,384]{1,0:T(8,128)(2,1)} %get-tuple-element.2612) | copy-start | bytes 884740 | tf_op jit(solution)/shard_map/while
  281.8 7.4 %copy-start.30 = (bf16[2,128,384]{1,2,0:T(8,128)(2,1)}, bf16[2,128,384]{1,2,0:T(8,128)(2,1)S(1)}, u32[]{:S(2)}) copy-start(bf16[2,128,384]{1,2,0:T(8,128)(2,1)S(1)} %copy.164) | copy-start | bytes 589828 | tf_op jit(solution)/shard_map/while
  290.2 5.4 copy-start.15
  318.0 7.5 %copy-start.46 = (bf16[4,128,384]{2,1,0:T(8,128)(2,1)}, bf16[4,128,384]{2,1,0:T(8,128)(2,1)S(1)}, u32[]{:S(2)}) copy-start(bf16[4,128,384]{2,1,0:T(8,128)(2,1)S(1)} %get-tuple-element.2622) | copy-start | bytes 1179652 | tf_op jit(solution)/shard_map/while
  327.3 5.2 copy-start.86
  329.6 7.7 %copy-start.23 = (bf16[384,384]{1,0:T(8,128)(2,1)S(1)}, bf16[384,384]{1,0:T(8,128)(2,1)}, u32[]{:S(2)}) copy-start(bf16[384,384]{1,0:T(8,128)(2,1)} %get-tuple-element.2612) | copy-start | bytes 884740 | tf_op jit(solution)/shard_map/while
  332.5 7.4 %copy-start.30 = (bf16[2,128,384]{1,2,0:T(8,128)(2,1)}, bf16[2,128,384]{1,2,0:T(8,128)(2,1)S(1)}, u32[]{:S(2)}) copy-start(bf16[2,128,384]{1,2,0:T(8,128)(2,1)S(1)} %copy.164) | copy-start | bytes 589828 | tf_op jit(solution)/shard_map/while
  340.9 5.4 copy-start.15
  354.9 5.8 copy-start.58
  356.1 4.6 copy-start.54
  356.1 5.6 copy-start.10
  366.1 4.1 copy-start.65
  372.8 5.8 copy-start.12
  (212 other events, 424.1 us)
Sparse Core Ops, SparseCore 0:
  11.0 56.8 all-gather.5
  70.7 54.4 all-gather.3
  128.3 56.1 all-gather.7
  392.6 215.2 all-reduce.7
where the time goes:
time: 621 us; the launch traced here: 619 us
  waiting for transfers between devices  299 us (48%)
  local copies, waits for them, and re-layouts  121 us (19%)
  blocking collectives  81.8 us (13%)
  matrix products  69.6 us (11%)
  other arithmetic  30.5 us (5%)
  between operations  14.7 us (2%)
    unnamed x5, waiting for transfers between devices  176 us
    unnamed x2, blocking collectives  81.8 us
    all_gather x1, waiting for transfers between devices, local(): lax.all_gather(mlp_weights, ('dp', 'fsdp'), axis=0, tiled=True)  55.6 us
    all_gather x1, waiting for transfers between devices, local(): lax.all_gather(ada_weights, ('dp', 'fsdp'), axis=0, tiled=True)  53.4 us
    dot_general x30, matrix products, mat_dot(): return jnp.dot(left, right, preferred_element_type=jnp.float32)  37.6 us
    dot_general x14, matrix products, product(): return jnp.einsum(form, left, right, preferred_element_type=jnp.float32)  32 us
    while x450, local copies, waits for them, and re-layouts  27.5 us
    dynamic_slice x20, local copies, waits for them, and re-layouts, take_rows(): return lax.dynamic_slice_in_dim(buffer, start, group_width, 0)  16.4 us
  transfers between devices with their start and end apart: 4, of which 4 were waited for; matrix products, arithmetic and copies ran while one was open for 1% of the time, Pallas kernels for 0%

commit v1 on v0

--- a/solution.py
+++ b/solution.py
@@ -1,8 +1,11 @@
 from functools import partial
+import math
 
 import jax
 import jax.numpy as jnp
 from jax import lax
+from jax.experimental import pallas as pl
+from jax.experimental.pallas import tpu as pltpu
 from jax.sharding import PartitionSpec as P
 
 FF = 1536
@@ -274,148 +277,343 @@
     )
 
 
-def empty_saved(slot_count, length, model_width, hidden_units, head_count):
-    plain = (slot_count, length, model_width)
-    wide = (slot_count, length, hidden_units)
-    column = (slot_count, length, 1)
-    return (
-        jnp.zeros((slot_count, model_width), jnp.bfloat16),
-        jnp.zeros((slot_count, 6 * model_width), jnp.float32),
-        jnp.zeros(plain, jnp.float32),
-        jnp.zeros(column, jnp.float32),
-        jnp.zeros(plain, jnp.bfloat16),
-        jnp.zeros(plain, jnp.bfloat16),
-        jnp.zeros(plain, jnp.bfloat16),
-        jnp.zeros(plain, jnp.bfloat16),
-        jnp.zeros((slot_count, head_count, length), jnp.float32),
-        jnp.zeros(plain, jnp.bfloat16),
-        jnp.zeros(plain, jnp.float32),
-        jnp.zeros(plain, jnp.float32),
-        jnp.zeros(column, jnp.float32),
-        jnp.zeros(plain, jnp.bfloat16),
-        jnp.zeros(wide, jnp.float32),
-        jnp.zeros(wide, jnp.bfloat16),
-        jnp.zeros(plain, jnp.float32),
-    )
-
-
-def take_rows(buffer, start, group_width):
-    return lax.dynamic_slice_in_dim(buffer, start, group_width, 0)
-
-
-def place_rows(buffer, piece, start):
-    return lax.dynamic_update_slice_in_dim(buffer, piece, start, 0)
-
-
-def zeros_for(weights, picks):
-    return tuple((jnp.zeros(weights[k].shape, jnp.float32) for k in picks))
-
-
-def add_terms(totals, terms):
-    return tuple((total + term for total, term in zip(totals, terms)))
+LANES = 128
+SUBLANES = 16
+AXES = ("dp", "fsdp")
+MESH = pl.DeviceIdType.MESH
+
+
+class Grid:
+    def __init__(self, mesh):
+        dp, fsdp = mesh.shape["dp"], mesh.shape["fsdp"]
+        side = math.isqrt(dp)
+        self.high = side if side * side == dp else 1
+        self.low = dp // self.high
+        self.pair = 2 if fsdp % 2 == 0 else 1
+        self.depth = fsdp // self.pair
+        self.count = dp * fsdp
+        self.sizes = (self.high, self.low, self.depth, self.pair)
+
+    def here(self):
+        a, f = lax.axis_index("dp"), lax.axis_index("fsdp")
+        return [a // self.low, a % self.low, f // self.pair, f % self.pair]
+
+    def peer(self, here, axis, step):
+        spot = list(here)
+        spot[axis] = lax.rem(here[axis] + step, self.sizes[axis])
+        return spot
+
+    def ident(self, spot):
+        return (spot[0] * self.low + spot[1], spot[2] * self.pair + spot[3])
+
+    def barrier(self, here):
+        sem = pltpu.get_barrier_semaphore()
+        total = 0
+        for axis in range(4):
+            for step in range(1, self.sizes[axis]):
+                pl.semaphore_signal(
+                    sem, inc=1, device_id=self.ident(self.peer(here, axis, step)), device_id_type=MESH
+                )
+                total += 1
+        pl.semaphore_wait(sem, total)
+
+
+def split_rows(rows, parts):
+    units = rows // SUBLANES
+    parts = min(parts, units)
+    cuts = [units * k // parts for k in range(parts + 1)]
+    return [(cuts[k] * SUBLANES, (cuts[k + 1] - cuts[k]) * SUBLANES) for k in range(parts)]
+
+
+def gather_kernel(grid, chunks, in_ref, out_ref, send_sem, recv_sem, own_sem):
+    here = grid.here()
+    hi, lo, z, c = here
+    spare = iter(range(send_sem.shape[0]))
+    grid.barrier(here)
+
+    def push(src, dst, spot):
+        k = next(spare)
+        copy = pltpu.make_async_remote_copy(
+            src_ref=src, dst_ref=dst, send_sem=send_sem.at[k], recv_sem=recv_sem.at[k],
+            device_id=grid.ident(spot), device_id_type=MESH,
+        )
+        copy.start()
+        return copy
+
+    def steps(axis):
+        return [grid.peer(here, axis, s) for s in range(1, grid.sizes[axis])]
+
+    everything = []
+
+    def pushes(src, dst, spots):
+        copies = [push(src, dst, spot) for spot in spots]
+        everything.extend(copies)
+        return copies
+
+    def arrive(copies):
+        for copy in copies:
+            copy.wait_recv()
+
+    own = pltpu.make_async_copy(in_ref, out_ref.at[hi, lo, z, c], own_sem)
+    own.start()
+    along_z, first, second, swap = [], [], [], []
+    for start, size in chunks:
+        rows = pl.ds(start, size)
+        along_z.append(pushes(in_ref.at[rows], out_ref.at[hi, lo, z, c, rows], steps(2)))
+    own.wait()
+    for k, (start, size) in enumerate(chunks):
+        rows = pl.ds(start, size)
+        arrive(along_z[k])
+        part = out_ref.at[hi, lo, :, c, rows]
+        first.append(pushes(part, part, steps(1 if k % 2 == 0 else 0)))
+        swap += pushes(part, part, steps(3))
+    for k, (start, size) in enumerate(chunks):
+        rows = pl.ds(start, size)
+        arrive(first[k])
+        if k % 2 == 0:
+            part = out_ref.at[hi, :, :, c, rows]
+            second.append(pushes(part, part, steps(0)))
+            others = [out_ref.at[hi, spot[1], :, c, rows] for spot in steps(1)]
+        else:
+            part = out_ref.at[:, lo, :, c, rows]
+            second.append(pushes(part, part, steps(1)))
+            others = [out_ref.at[spot[0], lo, :, c, rows] for spot in steps(0)]
+        for other in others:
+            swap += pushes(other, other, steps(3))
+    for k, (start, size) in enumerate(chunks):
+        rows = pl.ds(start, size)
+        arrive(second[k])
+        if k % 2 == 0:
+            others = [out_ref.at[spot[0], :, :, c, rows] for spot in steps(0)]
+        else:
+            others = [out_ref.at[:, spot[1], :, c, rows] for spot in steps(1)]
+        for other in others:
+            swap += pushes(other, other, steps(3))
+    arrive(swap)
+    for copy in everything:
+        copy.wait_send()
+
+
+def gather_copies(grid, chunk_count):
+    high, low, depth, pair = grid.sizes
+    first = lambda k: low - 1 if k % 2 == 0 else high - 1
+    second = lambda k: high - 1 if k % 2 == 0 else low - 1
+    return sum(
+        (depth - 1) + first(k) + second(k) + (pair - 1) * (1 + first(k) + second(k))
+        for k in range(chunk_count)
+    )
+
+
+def gather_all(grid, slab):
+    rows = slab.shape[0]
+    chunks = split_rows(rows, 4)
+    copies = gather_copies(grid, len(chunks))
+    return pl.pallas_call(
+        partial(gather_kernel, grid, chunks),
+        out_shape=jax.ShapeDtypeStruct(grid.sizes + slab.shape, slab.dtype),
+        in_specs=[pl.BlockSpec(memory_space=pltpu.VMEM)],
+        out_specs=pl.BlockSpec(memory_space=pltpu.VMEM),
+        scratch_shapes=[
+            pltpu.SemaphoreType.DMA((copies,)),
+            pltpu.SemaphoreType.DMA((copies,)),
+            pltpu.SemaphoreType.DMA,
+        ],
+        compiler_params=pltpu.CompilerParams(
+            collective_id=0, has_side_effects=True, vmem_limit_bytes=48 * 1024 * 1024
+        ),
+    )(slab)
+
+
+def scatter_kernel(
+    grid, chunks, g_ref, out_ref, pair_buf, acc, buf_one, buf_two, buf_z, send_sem, recv_sem
+):
+    here = grid.here()
+    hi, lo, z, c = here
+    spare = iter(range(send_sem.shape[0]))
+    grid.barrier(here)
+    everything = []
+
+    def push(src, dst, spot):
+        k = next(spare)
+        copy = pltpu.make_async_remote_copy(
+            src_ref=src, dst_ref=dst, send_sem=send_sem.at[k], recv_sem=recv_sem.at[k],
+            device_id=grid.ident(spot), device_id_type=MESH,
+        )
+        copy.start()
+        everything.append(copy)
+        return copy
+
+    def steps(axis):
+        return [(s - 1, grid.peer(here, axis, s)) for s in range(1, grid.sizes[axis])]
+
+    def arrive(copies):
+        for copy in copies:
+            copy.wait_recv()
+
+    def add(into, terms, first, second):
+        def body(t, _):
+            i, j = t // second, t % second
+            total = terms[0](i, j)[...].astype(jnp.float32)
+            for term in terms[1:]:
+                total = total + term(i, j)[...].astype(jnp.float32)
+            target = into(i, j)
+            target[...] = total.astype(target.dtype)
+            return 0
+
+        lax.fori_loop(0, first * second, body, 0)
+
+    high, low, depth, pair = grid.sizes
+    swaps, ones, twos, lines = [], [], [], []
+    for start, size in chunks:
+        rows = pl.ds(start, size)
+        swaps.append(
+            [push(g_ref.at[:, :, :, spot[3], rows], pair_buf.at[:, :, :, rows], spot) for _, spot in steps(3)]
+        )
+    for k, (start, size) in enumerate(chunks):
+        rows = pl.ds(start, size)
+        arrive(swaps[k])
+        terms = [lambda i, j: g_ref.at[i // low, i % low, j, c, rows]]
+        if pair > 1:
+            terms.append(lambda i, j: pair_buf.at[i // low, i % low, j, rows])
+        add(lambda i, j: acc.at[i // low, i % low, j, rows], terms, high * low, depth)
+        if k % 2 == 0:
+            ones.append(
+                [push(acc.at[spot[0], :, :, rows], buf_one.at[s, 0:low, :, rows], spot) for s, spot in steps(0)]
+            )
+        else:
+            ones.append(
+                [push(acc.at[:, spot[1], :, rows], buf_one.at[s, 0:high, :, rows], spot) for s, spot in steps(1)]
+            )
+    for k, (start, size) in enumerate(chunks):
+        rows = pl.ds(start, size)
+        arrive(ones[k])
+        even = k % 2 == 0
+        mine = (lambda i, j: acc.at[hi, i, j, rows]) if even else (lambda i, j: acc.at[i, lo, j, rows])
+        terms = [mine] + [
+            (lambda i, j, s=s: buf_one.at[s, i, j, rows]) for s, _ in steps(0 if even else 1)
+        ]
+        add(mine, terms, low if even else high, depth)
+        if even:
+            twos.append(
+                [push(acc.at[hi, spot[1], :, rows], buf_two.at[s, :, rows], spot) for s, spot in steps(1)]
+            )
+        else:
+            twos.append(
+                [push(acc.at[spot[0], lo, :, rows], buf_two.at[s, :, rows], spot) for s, spot in steps(0)]
+            )
+    for k, (start, size) in enumerate(chunks):
+        rows = pl.ds(start, size)
+        arrive(twos[k])
+        mine = lambda i, j: acc.at[hi, lo, j, rows]
+        terms = [mine] + [
+            (lambda i, j, s=s: buf_two.at[s, j, rows]) for s, _ in steps(1 if k % 2 == 0 else 0)
+        ]
+        add(mine, terms, 1, depth)
+        lines.append(
+            [push(acc.at[hi, lo, spot[2], rows], buf_z.at[s, rows], spot) for s, spot in steps(2)]
+        )
+    for k, (start, size) in enumerate(chunks):
+        rows = pl.ds(start, size)
+        arrive(lines[k])
+        total = acc[hi, lo, z, rows].astype(jnp.float32)
+        for s in range(depth - 1):
+            total = total + buf_z[s, rows].astype(jnp.float32)
+        out_ref[rows, :] = total
+    for copy in everything:
+        copy.wait_send()
+
+
+def scatter_sum(grid, packed):
+    high, low, depth, pair = grid.sizes
+    rows, lanes = packed.shape[-2:]
+    chunks = split_rows(rows, 4)
+    copies = len(chunks) * (high + low + depth + pair - 4)
+    kind = packed.dtype
+    return pl.pallas_call(
+        partial(scatter_kernel, grid, chunks),
+        out_shape=jax.ShapeDtypeStruct((rows, lanes), jnp.float32),
+        in_specs=[pl.BlockSpec(memory_space=pltpu.VMEM)],
+        out_specs=pl.BlockSpec(memory_space=pltpu.VMEM),
+        scratch_shapes=[
+            pltpu.VMEM((high, low, depth, rows, lanes), kind),
+            pltpu.VMEM((high, low, depth, rows, lanes), kind),
+            pltpu.VMEM((max(high, low) - 1, max(high, low), depth, rows, lanes), kind),
+            pltpu.VMEM((max(high, low) - 1, depth, rows, lanes), kind),
+            pltpu.VMEM((max(depth - 1, 1), rows, lanes), kind),
+            pltpu.SemaphoreType.DMA((copies,)),
+            pltpu.SemaphoreType.DMA((copies,)),
+        ],
+        compiler_params=pltpu.CompilerParams(
+            collective_id=1, has_side_effects=True, vmem_limit_bytes=48 * 1024 * 1024
+        ),
+    )(packed)
+
+
+def padded_rows(extent):
+    return -(-extent // LANES)
+
+
+def pack(pieces, lead):
+    parts = []
+    for piece in pieces:
+        extent = piece.shape[-1]
+        rows = padded_rows(extent)
+        gap = rows * LANES - extent
+        if gap:
+            piece = jnp.pad(piece, [(0, 0)] * len(lead) + [(0, gap)])
+        parts.append(piece.reshape(lead + (rows, LANES)))
+    total = sum(part.shape[-2] for part in parts)
+    gap = -total % SUBLANES
+    if gap:
+        parts.append(jnp.zeros(lead + (gap, LANES), parts[0].dtype))
+    return jnp.concatenate(parts, axis=-2)
 
 
 def local(
-    latents, conditioning, counts, cotangent, ada_weights, attn_weights, mlp_weights, flat_biases
+    grid, latents, conditioning, counts, cotangent, ada_weights, attn_weights, mlp_weights, flat_biases
 ):
     slot_count, length, model_width = latents.shape
-    group_width = 2
-    mlp_picks = (3, 4, 9, 10)
-    attn_picks = (0, 1, 2, 5, 6, 7, 8)
-    gathered = (
-        lax.all_gather(ada_weights, ("dp", "fsdp"), axis=0, tiled=True),
-        lax.all_gather(attn_weights, ("dp", "fsdp"), axis=0, tiled=True),
-        lax.all_gather(mlp_weights, ("dp", "fsdp"), axis=0, tiled=True),
-        lax.all_gather(flat_biases, ("dp", "fsdp"), axis=0, tiled=True),
-    )
-    weights = unpack(gathered[0], gathered[1], gathered[2], gathered[3], model_width, FF)
-    own_count = counts[0]
-    live = jnp.arange(slot_count, dtype=jnp.int32) < own_count
-    turns = slot_count // group_width
-
-    def forward_step(turn, carry):
-        out_buffer, saved_buffer = carry
-        start = turn * group_width
-        output, saved = forward_group(
-            take_rows(latents, start, group_width),
-            take_rows(conditioning, start, group_width),
-            take_rows(live, start, group_width),
-            weights,
-            HEADS,
+    shards = (ada_weights, attn_weights, mlp_weights, flat_biases)
+    gathered = gather_all(grid, pack(shards, ()))
+    gathered = gathered.reshape((grid.count,) + gathered.shape[-2:])
+    flats, row = [], 0
+    for shard in shards:
+        extent = shard.shape[0]
+        rows = padded_rows(extent)
+        flats.append(
+            gathered[:, row : row + rows].reshape(grid.count, rows * LANES)[:, :extent].reshape(-1)
         )
-        saved_buffer = jax.tree.map(partial(place_rows, start=start), saved_buffer, saved)
-        return (place_rows(out_buffer, output, start), saved_buffer)
-
-    start_state = (
-        jnp.zeros(latents.shape, jnp.float32),
-        empty_saved(slot_count, length, model_width, FF, HEADS),
-    )
-    out_buffer, saved_buffer = lax.fori_loop(0, turns, forward_step, start_state)
-    again = (
-        lax.all_gather(ada_weights, ("dp", "fsdp"), axis=0, tiled=True),
-        lax.all_gather(attn_weights, ("dp", "fsdp"), axis=0, tiled=True),
-        lax.all_gather(mlp_weights, ("dp", "fsdp"), axis=0, tiled=True),
-        lax.all_gather(flat_biases, ("dp", "fsdp"), axis=0, tiled=True),
-    )
-    back_weights = unpack(again[0], again[1], again[2], again[3], model_width, FF)
-
-    def saved_rows(start):
-        return jax.tree.map(partial(take_rows, start=start, group_width=group_width), saved_buffer)
-
-    def both_step(turn, carry):
-        grad_buffer, cond_buffer, attn_totals, mlp_totals = carry
-        start = turn * group_width
-        saved_piece = saved_rows(start)
-        grad_after, mod_tail, mlp_terms = mlp_backward(
-            saved_piece,
-            take_rows(cotangent, start, group_width),
-            take_rows(live, start, group_width),
-            back_weights,
-        )
-        grad_input, grad_cond, attn_terms = attention_backward(
-            saved_piece,
-            take_rows(conditioning, start, group_width),
-            grad_after,
-            mod_tail,
-            back_weights,
-            HEADS,
-        )
-        return (
-            place_rows(grad_buffer, grad_input, start),
-            place_rows(cond_buffer, grad_cond, start),
-            add_terms(attn_totals, attn_terms),
-            add_terms(mlp_totals, mlp_terms),
-        )
-
-    both_state = (
-        jnp.zeros(latents.shape, jnp.float32),
-        jnp.zeros(conditioning.shape, jnp.float32),
-        zeros_for(back_weights, attn_picks),
-        zeros_for(back_weights, mlp_picks),
-    )
-    grad_latents, grad_conditioning, attn_totals, mlp_totals = lax.fori_loop(
-        0, turns, both_step, both_state
-    )
-    ada_terms = attn_totals[0].reshape(-1)
-    attn_flat_terms = jnp.concatenate([attn_totals[1].reshape(-1), attn_totals[2].reshape(-1)])
-    mlp_flat_terms = jnp.concatenate([mlp_totals[0].reshape(-1), mlp_totals[1].reshape(-1)])
-    bias_terms = jnp.concatenate(
+        row += rows
+    weights = unpack(flats[0], flats[1], flats[2], flats[3], model_width, FF)
+    live = jnp.arange(slot_count, dtype=jnp.int32) < counts[0]
+    output, saved = forward_group(latents, conditioning, live, weights, HEADS)
+    grad_after, mod_tail, mlp_terms = mlp_backward(saved, cotangent, live, weights)
+    grad_latents, grad_conditioning, attn_terms = attention_backward(
+        saved, conditioning, grad_after, mod_tail, weights, HEADS
+    )
+
+    def flat(*terms):
+        return jnp.concatenate(
+            [term.astype(jnp.bfloat16).reshape(-1) for term in terms]
+        ).reshape(grid.count, -1)
+
+    packed = pack(
         [
-            attn_totals[3],
-            attn_totals[4],
-            attn_totals[5],
-            attn_totals[6],
-            mlp_totals[2],
-            mlp_totals[3],
-        ]
-    )
-    grad_ada, grad_attn, grad_mlp, grad_biases = (
-        lax.psum_scatter(ada_terms, ("dp", "fsdp"), scatter_dimension=0, tiled=True),
-        lax.psum_scatter(attn_flat_terms, ("dp", "fsdp"), scatter_dimension=0, tiled=True),
-        lax.psum_scatter(mlp_flat_terms, ("dp", "fsdp"), scatter_dimension=0, tiled=True),
-        lax.psum_scatter(bias_terms, ("dp", "fsdp"), scatter_dimension=0, tiled=True),
-    )
-    return (out_buffer, grad_latents, grad_conditioning, grad_ada, grad_attn, grad_mlp, grad_biases)
+            flat(attn_terms[0]),
+            flat(attn_terms[1], attn_terms[2]),
+            flat(mlp_terms[0], mlp_terms[1]),
+            flat(attn_terms[3], attn_terms[4], attn_terms[5], attn_terms[6], mlp_terms[2], mlp_terms[3]),
+        ],
+        (grid.count,),
+    )
+    summed = scatter_sum(grid, packed.reshape(grid.sizes + packed.shape[1:]))
+    grads, row = [], 0
+    for shard in shards:
+        extent = shard.shape[0]
+        rows = padded_rows(extent)
+        grads.append(summed[row : row + rows].reshape(-1)[:extent])
+        row += rows
+    return (output, grad_latents, grad_conditioning) + tuple(grads)
 
 
 def solution(mesh):
@@ -438,4 +636,4 @@
         P(("dp", "fsdp")),
         P(("dp", "fsdp")),
     )
-    return jax.shard_map(local, mesh=mesh, in_specs=in_specs, out_specs=out_specs, check_vma=False)
+    return jax.shard_map(partial(local, Grid(mesh)), mesh=mesh, in_specs=in_specs, out_specs=out_specs, check_vma=False)

time: 621 us -> 253 us (0.41)
  waiting for transfers between devices: 299 us -> 0 us
  Pallas kernels: 0 us -> 85.1 us
  blocking collectives: 81.8 us -> 0 us
  local copies, waits for them, and re-layouts: 121 us -> 98 us
  matrix products: 69.6 us -> 51.3 us
  other arithmetic: 30.5 us -> 14.6 us
  between operations: 14.7 us -> 1.82 us
    unnamed x5 -> x0, waiting for transfers between devices: 176 us -> none
    all_gather x3 -> x0, waiting for transfers between devices: 122 us -> none  [the longest x1 55.6 us: local(): lax.all_gather(mlp_weights, ('dp', 'fsdp'), axis=0, tiled=True)]
    pallas_call x0 -> x2, Pallas kernels: none -> 85.1 us  [the longest x1 43.6 us: scatter_sum(): pl.pallas_call(partial(scatter_kernel, grid, chunks), out_shape=jax.Shape...]
    unnamed x2 -> x0, blocking collectives: 81.8 us -> none
    concatenate x1 -> x7, local copies, waits for them, and re-layouts: 0.01 us -> 32.1 us  [the longest x4 27 us: pack(): return jnp.concatenate(parts, axis=-2)]
    while x450 -> x0, local copies, waits for them, and re-layouts: 27.5 us -> none
    dynamic_slice x20 -> x0, local copies, waits for them, and re-layouts: 16.4 us -> none  [take_rows(): return lax.dynamic_slice_in_dim(buffer, start, group_width, 0)]
    dot_general x14 -> x6, matrix products: 32 us -> 19.5 us  [product(): return jnp.einsum(form, left, right, preferred_element_type=jnp.float32)]
  transfers between devices with their start and end apart: 4 -> 0, of which waited for: 4 -> 0; matrix products, arithmetic and copies ran while one was open for 1% -> 0% of each run, Pallas kernels for 0% -> 0%
where the time goes in v1:
time: 253 us; the launch traced here: 251 us
  local copies, waits for them, and re-layouts  98 us (39%)
  Pallas kernels  85.1 us (34%)
  matrix products  51.3 us (20%)
  other arithmetic  14.6 us (6%)
    pallas_call x1, Pallas kernels, scatter_sum(): pl.pallas_call(partial(scatter_kernel, grid, chunks), out_shape=jax.Shape...  43.6 us
    pallas_call x1, Pallas kernels, gather_all(): pl.pallas_call(partial(gather_kernel, grid, chunks), out_shape=jax.ShapeD...  41.5 us
    dot_general x15, matrix products, mat_dot(): return jnp.dot(left, right, preferred_element_type=jnp.float32)  31.8 us
    concatenate x4, local copies, waits for them, and re-layouts, pack(): return jnp.concatenate(parts, axis=-2)  27 us
    dot_general x6, matrix products, product(): return jnp.einsum(form, left, right, preferred_element_type=jnp.float32)  19.5 us
    unnamed x74, local copies, waits for them, and re-layouts  16.9 us
    reshape x2, local copies, waits for them, and re-layouts, unpack(): mlp_flat[:fc1_size].reshape(model_width, hidden_units)  6.93 us
    concatenate x3, local copies, waits for them, and re-layouts, attention_backward(): grad_proj_in = jnp.concatenate([grad_query, grad_key, grad_value], axis=1)  5.75 us

profile of v1, /device:TPU:0, one launch (start us, length us, event | category | flops | bytes accessed | tf_op | source)
XLA Modules:
  0.0 250.8 jit_solution(18359350421493376839)
XLA Ops:
  1.3 2.5 %concatenate.44.in_ref = bf16[656,128]{1,0:T(8,128)(2,1)S(1)} concatenate(bf16[216,128]{1,0:T(8,128)(2,1)} %bitcast.138, bf16[144,128]{1,0:T(8,128)(2,1)} %bitcast.139, bf16[288,128]{1,0:T(8,128)(2,1)} %bitcast.135, bf16[2,128]{1,0:T(2,128)(2,1)S(1)} %pad_bitcast_fusion, bf16[6,128]{1,0:T(8,128)(2,1)S(1)} %broadcast_in_dim.17), dimensions={0} | concatenate | bytes 335872 | tf_op jit(solution)/shard_map/concatenate | solution.py:569
  3.8 41.5 %shard_map.135 = bf16[2,2,4,2,656,128]{5,4,3,2,1,0:T(8,128)(2,1)S(1)} custom-call(bf16[656,128]{1,0:T(8,128)(2,1)S(1)} %concatenate.44.in_ref), custom_call_target="tpu_custom_call" | custom-call | tf_op jit(solution)/shard_map/pallas_call | solution.py:411
  45.4 2.3 copy-done.1
  63.4 2.4 fusion.39
  71.5 2.7 %fusion.26 = bf16[4,128,6,64]{1,3,2,0:T(8,128)(2,1)S(1)} fusion(f32[4,6,128,128]{2,3,1,0:T(8,128)} %convolution_multiply_fusion.1, bf16[4,128,6,64]{1,0,3,2:T(4,128)(2,1)} %reshape_reshape.6), kind=kOutput, calls=%fused_computation.36 | convolution fusion | flops 51317888 | bytes 2359296 | tf_op jit(solution)/shard_map/ghqk,gkhe->gqhe/dot_general | solution.py:50
  77.1 3.2 %fusion.76 = (bf16[16,288,128]{2,1,0:T(8,128)(2,1)}, bf16[16,288,128]{2,1,0:T(8,128)(2,1)}) fusion(bf16[32,656,128]{2,1,0:T(8,128)(2,1)} %bitcast.109), kind=kLoop, calls=%fused_computation.141 | loop fusion | bytes 4718592 | tf_op jit(solution)/shard_map/slice | solution.py:64
  80.3 3.5 %reshape.215 = bf16[384,1536]{1,0:T(8,128)(2,1)} reshape(bf16[16,288,128]{2,1,0:T(8,128)(2,1)} %get-tuple-element.22) | data formatting | bytes 2359296 | tf_op jit(solution)/shard_map/reshape | solution.py:64
  83.8 4.0 %convolution_add_fusion = f32[512,1536]{1,0:T(8,128)} fusion(bf16[512,384]{1,0:T(8,128)(2,1)} %bitcast.133, bf16[384,1536]{1,0:T(8,128)(2,1)} %reshape.215, f32[1536]{0:T(1024)S(1)} %slice_convert_fusion.2), kind=kOutput, calls=%fused_computation.6 | convolution fusion | flops 604766208 | bytes 4724736 | tf_op jit(solution)/shard_map/dot_general | solution.py:54
  88.5 3.1 %reshape.216 = bf16[1536,384]{1,0:T(8,128)(2,1)} reshape(bf16[16,288,128]{2,1,0:T(8,128)(2,1)} %get-tuple-element.23) | data formatting | bytes 2359296 | tf_op jit(solution)/shard_map/reshape | solution.py:65
  91.6 4.7 %multiply_reduce_fusion.10 = (bf16[384]{0:T(512)(128)(2,1)S(1)}, f32[4,384]{1,0:T(4,128)S(1)}, bf16[4,128,384]{2,1,0:T(8,128)(2,1)S(1)}, f32[512,384]{1,0:T(8,128)}) fusion(f32[4,128,384]{2,1,0:T(8,128)} %param.11, f32[4,384]{1,0:T(4,128)S(1)} %get-tuple-element.30, pred[4]{0:T(512)(128)(4,1)S(1)} %iota_compare_fusion, f32[384]{0:T(512)S(1)} %get-tuple-element.36, ...), kind=kOutput, calls=%fused_computation.73 | convolution fusion | flops 612432000 | bytes 6306052 | tf_op jit(solution)/shard_map/dot_general | solution.py:54
  96.3 3.9 %fusion.77 = (bf16[1536]{0:T(1024)(128)(2,1)}, bf16[512,1536]{1,0:T(8,128)(2,1)}) fusion(f32[512,1536]{1,0:T(8,128)S(1)} %copy-done.9, bf16[512,384]{1,0:T(8,128)(2,1)S(1)} %bitcast.128, bf16[1536,384]{1,0:T(8,128)(2,1)S(1)} %copy-done.8), kind=kOutput, calls=%fused_computation.142 | convolution fusion | flops 619706880 | bytes 6294528 | tf_op jit(solution)/shard_map/dot_general | solution.py:54
  100.2 3.5 %reshape.231 = bf16[384,1536,1]{1,0,2:T(8,128)(2,1)} reshape(bf16[16,288,128]{2,1,0:T(8,128)(2,1)} %get-tuple-element.22) | data formatting | bytes 2359296 | tf_op jit(solution)/shard_map/reshape | solution.py:64
  103.7 3.1 %multiply_reduce_fusion.2 = (f32[4,384]{1,0:T(4,128)S(1)}, f32[4,128]{1,0:T(4,128)S(1)}, f32[4,128]{1,0:T(4,128)S(1)}, f32[4,384]{1,0:T(4,128)S(1)}, f32[4,128,384]{2,1,0:T(8,128)S(1)}) fusion(f32[4,128,384]{2,1,0:T(8,128)S(1)} %get-tuple-element.21, f32[4,128]{1,0:T(4,128)S(1)} %add_rsqrt_fusion, f32[4,128]{1,0:T(4,128)S(1)} %broadcast_multiply_fusion.4, ...), kind=kOutput, calls=%fused_computation.56 | convolution fusion | flops 605745152 | bytes 4352000 | tf_op jit(solution)/shard_map/dot_general | solution.py:54
  108.6 3.0 %reshape.232 = bf16[384,1152,1]{1,0,2:T(8,128)(2,1)} reshape(bf16[24,144,128]{2,1,0:T(8,128)(2,1)} %copy-done.3) | data formatting | bytes 1769472 | tf_op jit(solution)/shard_map/reshape | solution.py:62
  118.3 4.0 %bitcast_reduce_fusion = (bf16[6,64]{1,0:T(8,128)(2,1)}, bf16[4,6,64,128]{3,2,1,0:T(8,128)(2,1)}) fusion(f32[4,6,128,128]{2,3,1,0:T(8,128)} %convolution_multiply_fusion.1, bf16[4,128,6,64]{1,0,3,2:T(4,128)(2,1)} %reshape.220), kind=kOutput, calls=%fused_computation.136 | convolution fusion | flops 51514112 | bytes 2360064 | tf_op jit(solution)/shard_map/ghqk,gqhe->gkhe/dot_general | solution.py:50
  124.2 3.6 %fusion.7 = f32[4,6,128,128]{2,3,1,0:T(8,128)} fusion(f32[4,6,128,128]{2,3,1,0:T(8,128)} %convolution_multiply_fusion.1), kind=kOutput, calls=%fused_computation.19 | output fusion | flops 396415 | bytes 3145728 | tf_op jit(solution)/shard_map/reduce_sum | solution.py:114
  129.4 4.5 %fusion.23 = bf16[4,6,64,128]{3,2,1,0:T(8,128)(2,1)} fusion(f32[4,6,128,128]{2,3,1,0:T(8,128)} %fusion.7, f32[4,6,128,128]{2,3,1,0:T(8,128)} %fusion.57, bf16[4,128,6,64]{1,0,3,2:T(4,128)(2,1)} %copy-done.15), kind=kOutput, calls=%fused_computation.31 | convolution fusion | flops 52497536 | bytes 3932160 | tf_op jit(solution)/shard_map/ghqk,gqhe->gkhe/dot_general | solution.py:50
  135.8 5.1 %bitcast_reduce_fusion.1 = (bf16[6,64]{1,0:T(8,128)(2,1)}, bf16[4,6,64,128]{3,2,1,0:T(8,128)(2,1)}) fusion(f32[4,6,128,128]{2,3,1,0:T(8,128)} %fusion.7, f32[4,6,128,128]{2,3,1,0:T(8,128)} %fusion.57, bf16[4,128,6,64]{1,0,3,2:T(4,128)(2,1)} %copy-done.14), kind=kOutput, calls=%fused_computation.137 | convolution fusion | flops 52693760 | bytes 3932928 | tf_op jit(solution)/shard_map/ghqk,gkhe->gqhe/dot_general | solution.py:50
  142.8 2.6 %multiply_reduce_fusion.4 = (f32[4,384]{1,0:T(4,128)S(1)}, f32[4,128]{1,0:T(4,128)S(1)}, f32[4,128]{1,0:T(4,128)S(1)}, f32[4,384]{1,0:T(4,128)S(1)}, f32[4,128,384]{2,1,0:T(8,128)S(1)}) fusion(f32[4,128,384]{2,1,0:T(8,128)S(1)} %copy-done.2, f32[4,128]{1,0:T(4,128)S(1)} %add_rsqrt_fusion.1, f32[4,128]{1,0:T(4,128)S(1)} %broadcast_multiply_fusion.5, ...), kind=kOutput, calls=%fused_computation.58 | convolution fusion | flops 458289152 | bytes 3663872 | tf_op jit(solution)/shard_map/dot_general | solution.py:54
  148.6 3.1 %concatenate.50 = bf16[2,2,4,2,216,128]{5,4,3,2,1,0:T(8,128)(2,1)} reshape(bf16[384,2304]{1,0:T(8,128)(2,1)S(1)} %convolution_convert_fusion) | data formatting | bytes 3538944 | tf_op jit(solution)/shard_map/concatenate | solution.py:569
  156.8 3.3 %convolution_convert_fusion.1 = bf16[1536,384]{1,0:T(8,128)(2,1)S(1)} fusion(bf16[512,384]{1,0:T(8,128)(2,1)S(1)} %bitcast.129, f32[512,1536]{1,0:T(8,128)} %convolution_add_fusion), kind=kOutput, calls=%fused_computation.14 | convolution fusion | flops 611647488 | bytes 4718592 | tf_op jit(solution)/shard_map/dot_general | solution.py:54
  181.4 20.7 %concatenate.60.g_ref = bf16[2,2,4,2,656,128]{5,4,3,2,1,0:T(8,128)(2,1)} concatenate(bf16[2,2,4,2,216,128]{5,4,3,2,1,0:T(8,128)(2,1)} %concatenate.50, bf16[2,2,4,2,144,128]{5,4,3,2,1,0:T(8,128)(2,1)S(1)} %bitcast.112, bf16[2,2,4,2,288,128]{5,4,3,2,1,0:T(8,128)(2,1)S(1)} %bitcast.110, bf16[2,2,4,2,2,128]{5,4,3,2,1,0:T(2,128)(2,1)S(1)} %concatenate.59, ...), dimensions={4} | concatenate | bytes 10747904 | tf_op jit(solution)/shard_map/concatenate | solution.py:569
  202.1 2.5 %copy-done = bf16[2,2,4,2,656,128]{5,4,3,2,1,0:T(8,128)(2,1)S(1)} copy-done((bf16[2,2,4,2,656,128]{5,4,3,2,1,0:T(8,128)(2,1)S(1)}, bf16[2,2,4,2,656,128]{5,4,3,2,1,0:T(8,128)(2,1)}, u32[]{:S(2)}) %copy-start) | copy-done | bytes 5373976
  204.6 43.6 %shard_map.136 = f32[656,128]{1,0:T(8,128)S(1)} custom-call(bf16[2,2,4,2,656,128]{5,4,3,2,1,0:T(8,128)(2,1)S(1)} %copy-done), custom_call_target="tpu_custom_call" | custom-call | tf_op jit(solution)/shard_map/pallas_call | solution.py:532
  (150 shorter events, 72.6 us)
Async XLA Ops:
  45.3 2.3 copy-start.1
  47.8 3.1 %copy-start.29 = (f32[4,384]{1,0:T(4,128)S(1)}, f32[4,384]{1,0:T(4,128)}, u32[]{:S(2)}) copy-start(f32[4,384]{1,0:T(4,128)} %param.9) | copy-start | bytes 18436
  50.8 2.3 copy-start.2
  55.7 4.1 %copy-start.3 = (bf16[24,144,128]{2,1,0:T(8,128)(2,1)}, bf16[24,144,128]{2,1,0:T(8,128)(2,1)S(1)}, u32[]{:S(2)}) copy-start(bf16[24,144,128]{2,1,0:T(8,128)(2,1)S(1)} %slice.130) | copy-start | bytes 2654212
  59.8 1.4 copy-start.4
  63.3 4.4 %copy-start.14 = (bf16[4,128,6,64]{1,0,3,2:T(4,128)(2,1)}, bf16[4,128,6,64]{1,0,3,2:T(4,128)(2,1)S(1)}, u32[]{:S(2)}) copy-start(bf16[4,128,6,64]{1,0,3,2:T(4,128)(2,1)S(1)} %reshape_reshape.8) | copy-start | bytes 1179652
  67.8 2.8 %copy-start.15 = (bf16[4,128,6,64]{1,0,3,2:T(4,128)(2,1)}, bf16[4,128,6,64]{1,0,3,2:T(4,128)(2,1)S(1)}, u32[]{:S(2)}) copy-start(bf16[4,128,6,64]{1,0,3,2:T(4,128)(2,1)S(1)} %reshape_reshape.7) | copy-start | bytes 1179652
  71.5 3.0 %copy-start.12 = (bf16[384,384]{1,0:T(8,128)(2,1)S(1)}, bf16[384,384]{1,0:T(8,128)(2,1)}, u32[]{:S(2)}) copy-start(bf16[384,384]{1,0:T(8,128)(2,1)} %reshape.212) | copy-start | bytes 884740
  91.6 4.7 %copy-start.8 = (bf16[1536,384]{1,0:T(8,128)(2,1)S(1)}, bf16[1536,384]{1,0:T(8,128)(2,1)}, u32[]{:S(2)}) copy-start(bf16[1536,384]{1,0:T(8,128)(2,1)} %reshape.216) | copy-start | bytes 3538948
  91.6 4.7 %copy-start.9 = (f32[512,1536]{1,0:T(8,128)S(1)}, f32[512,1536]{1,0:T(8,128)}, u32[]{:S(2)}) copy-start(f32[512,1536]{1,0:T(8,128)} %convolution_add_fusion) | copy-start | bytes 9437188
  96.3 4.0 %copy-start.25 = (bf16[4,128,384]{2,1,0:T(8,128)(2,1)}, bf16[4,128,384]{2,1,0:T(8,128)(2,1)S(1)}, u32[]{:S(2)}) copy-start(bf16[4,128,384]{2,1,0:T(8,128)(2,1)S(1)} %get-tuple-element.28) | copy-start | bytes 1179652
  103.7 3.1 %copy-start.6 = (f32[512,384]{1,0:T(8,128)S(1)}, f32[512,384]{1,0:T(8,128)}, u32[]{:S(2)}) copy-start(f32[512,384]{1,0:T(8,128)} %copy-done.5) | copy-start | bytes 2359300
  103.7 3.1 %copy-start.10 = (f32[4,128,384]{2,1,0:T(8,128)S(1)}, f32[4,128,384]{2,1,0:T(8,128)}, u32[]{:S(2)}) copy-start(f32[4,128,384]{2,1,0:T(8,128)} %param.11) | copy-start | bytes 2359300
  103.7 3.1 %copy-start.11 = (f32[512,384]{1,0:T(8,128)S(1)}, f32[512,384]{1,0:T(8,128)}, u32[]{:S(2)}) copy-start(f32[512,384]{1,0:T(8,128)} %get-tuple-element.40) | copy-start | bytes 2359300
  108.6 3.0 %copy-start.7 = (f32[4,128,384]{2,1,0:T(8,128)S(1)}, f32[4,128,384]{2,1,0:T(8,128)}, u32[]{:S(2)}) copy-start(f32[4,128,384]{2,1,0:T(8,128)} %get-tuple-element.19) | copy-start | bytes 2359300
  124.2 3.6 %copy-start.16 = (bf16[4,128,6,64]{1,0,3,2:T(4,128)(2,1)S(1)}, bf16[4,128,6,64]{1,0,3,2:T(4,128)(2,1)}, u32[]{:S(2)}) copy-start(bf16[4,128,6,64]{1,0,3,2:T(4,128)(2,1)} %reshape_reshape.6) | copy-start | bytes 1179652
  124.2 3.6 %copy-start.20 = (bf16[4,128,6,64]{1,0,3,2:T(4,128)(2,1)S(1)}, bf16[4,128,6,64]{1,0,3,2:T(4,128)(2,1)}, u32[]{:S(2)}) copy-start(bf16[4,128,6,64]{1,0,3,2:T(4,128)(2,1)} %reshape.220) | copy-start | bytes 1179652
  146.7 1.2 copy-start.28
  148.6 3.1 %copy-start.22 = (bf16[4,128,6,64]{1,0,3,2:T(4,128)(2,1)S(1)}, bf16[4,128,6,64]{1,0,3,2:T(4,128)(2,1)}, u32[]{:S(2)}) copy-start(bf16[4,128,6,64]{1,0,3,2:T(4,128)(2,1)} %copy-done.21) | copy-start | bytes 1179652
  148.6 3.1 %copy-start.24 = (bf16[4,128,384]{2,1,0:T(8,128)(2,1)S(1)}, bf16[4,128,384]{2,1,0:T(8,128)(2,1)}, u32[]{:S(2)}) copy-start(bf16[4,128,384]{2,1,0:T(8,128)(2,1)} %copy-done.23) | copy-start | bytes 1179652
  151.7 1.4 copy-start.19
  153.1 1.0 copy-start.13
  160.0 1.4 copy-start.27
  202.1 2.5 %copy-start = (bf16[2,2,4,2,656,128]{5,4,3,2,1,0:T(8,128)(2,1)S(1)}, bf16[2,2,4,2,656,128]{5,4,3,2,1,0:T(8,128)(2,1)}, u32[]{:S(2)}) copy-start(bf16[2,2,4,2,656,128]{5,4,3,2,1,0:T(8,128)(2,1)} %concatenate.60.g_ref) | copy-start | bytes 16121860
  (6 other events, 5.4 us)

commit v2 on v1

v2 whole, which is shorter than its diff:
```python
from functools import partial
import math

import jax
import jax.numpy as jnp
from jax import lax
from jax.experimental import pallas as pl
from jax.experimental.pallas import tpu as pltpu
from jax.sharding import PartitionSpec as P

FF = 1536
HEADS = 6


EPSILON = 1e-06
GELU_COEF = 0.044715
ROOT_TWO_OVER_PI = 0.7978845608028654


def layer_norm(values):
    centre = values - jnp.mean(values, axis=-1, keepdims=True)
    inverse = lax.rsqrt(jnp.mean(centre * centre, axis=-1, keepdims=True) + EPSILON)
    return (centre * inverse, inverse)


def norm_backward(grad_norm, normed, inverse):
    first = jnp.mean(grad_norm, axis=-1, keepdims=True)
    second = jnp.mean(grad_norm * normed, axis=-1, keepdims=True)
    return (grad_norm - first - normed * second) * inverse


def gelu_value(pre_act):
    inner = ROOT_TWO_OVER_PI * (pre_act + GELU_COEF * pre_act * pre_act * pre_act)
    return 0.5 * pre_act * (1.0 + jnp.tanh(inner))


def gelu_slope(pre_act):
    tanh_part = jnp.tanh(ROOT_TWO_OVER_PI * (pre_act + GELU_COEF * pre_act * pre_act * pre_act))
    return 0.5 * (1.0 + tanh_part) + 0.5 * pre_act * (
        1.0 - tanh_part * tanh_part
    ) * ROOT_TWO_OVER_PI * (1.0 + 3.0 * GELU_COEF * pre_act * pre_act)


def silu_slope(values):
    sigma = jax.nn.sigmoid(values)
    return sigma * (1.0 + values * (1.0 - sigma))


def unpack(ada_flat, attn_flat, mlp_flat, bias_flat, model_width, hidden_units):
    qkv_size = 3 * model_width * model_width
    fc1_size = model_width * hidden_units
    pieces = [
        ada_flat.reshape(model_width, 6 * model_width),
        attn_flat[:qkv_size].reshape(model_width, 3 * model_width),
        attn_flat[qkv_size:].reshape(model_width, model_width),
        mlp_flat[:fc1_size].reshape(model_width, hidden_units),
        mlp_flat[fc1_size:].reshape(hidden_units, model_width),
    ]
    offset = 0
    for extent_now in [
        6 * model_width,
        model_width,
        model_width,
        model_width,
        hidden_units,
        model_width,
    ]:
        pieces.append(bias_flat[offset : offset + extent_now])
        offset = offset + extent_now
    return tuple(pieces)


LANES = 128
SUBLANES = 16
AXES = ("dp", "fsdp")
MESH = pl.DeviceIdType.MESH


class Grid:
    def __init__(self, mesh):
        dp, fsdp = mesh.shape["dp"], mesh.shape["fsdp"]
        side = math.isqrt(dp)
        self.high = side if side * side == dp else 1
        self.low = dp // self.high
        self.pair = 2 if fsdp % 2 == 0 else 1
        self.depth = fsdp // self.pair
        self.count = dp * fsdp
        self.sizes = (self.high, self.low, self.depth, self.pair)

    def here(self):
        a, f = lax.axis_index("dp"), lax.axis_index("fsdp")
        return [a // self.low, a % self.low, f // self.pair, f % self.pair]

    def peer(self, here, axis, step):
        spot = list(here)
        spot[axis] = lax.rem(here[axis] + step, self.sizes[axis])
        return spot

    def ident(self, spot):
        return (spot[0] * self.low + spot[1], spot[2] * self.pair + spot[3])

    def barrier(self, here):
        sem = pltpu.get_barrier_semaphore()
        total = 0
        for axis in range(4):
            for step in range(1, self.sizes[axis]):
                pl.semaphore_signal(
                    sem, inc=1, device_id=self.ident(self.peer(here, axis, step)), device_id_type=MESH
                )
                total += 1
        pl.semaphore_wait(sem, total)


def split_rows(rows, parts):
    units = rows // SUBLANES
    parts = min(parts, units)
    cuts = [units * k // parts for k in range(parts + 1)]
    return [(cuts[k] * SUBLANES, (cuts[k + 1] - cuts[k]) * SUBLANES) for k in range(parts)]


def gather_kernel(grid, chunks, in_ref, out_ref, send_sem, recv_sem, own_sem):
    here = grid.here()
    hi, lo, z, c = here
    spare = iter(range(send_sem.shape[0]))
    grid.barrier(here)

    def push(src, dst, spot):
        k = next(spare)
        copy = pltpu.make_async_remote_copy(
            src_ref=src, dst_ref=dst, send_sem=send_sem.at[k], recv_sem=recv_sem.at[k],
            device_id=grid.ident(spot), device_id_type=MESH,
        )
        copy.start()
        return copy

    def steps(axis):
        return [grid.peer(here, axis, s) for s in range(1, grid.sizes[axis])]

    everything = []

    def pushes(src, dst, spots):
        copies = [push(src, dst, spot) for spot in spots]
        everything.extend(copies)
        return copies

    def arrive(copies):
        for copy in copies:
            copy.wait_recv()

    own = pltpu.make_async_copy(in_ref, out_ref.at[hi, lo, z, c], own_sem)
    own.start()
    along_z, first, second, swap = [], [], [], []
    for start, size in chunks:
        rows = pl.ds(start, size)
        along_z.append(pushes(in_ref.at[rows], out_ref.at[hi, lo, z, c, rows], steps(2)))
    own.wait()
    for k, (start, size) in enumerate(chunks):
        rows = pl.ds(start, size)
        arrive(along_z[k])
        part = out_ref.at[hi, lo, :, c, rows]
        first.append(pushes(part, part, steps(1 if k % 2 == 0 else 0)))
        swap += pushes(part, part, steps(3))
    for k, (start, size) in enumerate(chunks):
        rows = pl.ds(start, size)
        arrive(first[k])
        if k % 2 == 0:
            part = out_ref.at[hi, :, :, c, rows]
            second.append(pushes(part, part, steps(0)))
            others = [out_ref.at[hi, spot[1], :, c, rows] for spot in steps(1)]
        else:
            part = out_ref.at[:, lo, :, c, rows]
            second.append(pushes(part, part, steps(1)))
            others = [out_ref.at[spot[0], lo, :, c, rows] for spot in steps(0)]
        for other in others:
            swap += pushes(other, other, steps(3))
    for k, (start, size) in enumerate(chunks):
        rows = pl.ds(start, size)
        arrive(second[k])
        if k % 2 == 0:
            others = [out_ref.at[spot[0], :, :, c, rows] for spot in steps(0)]
        else:
            others = [out_ref.at[:, spot[1], :, c, rows] for spot in steps(1)]
        for other in others:
            swap += pushes(other, other, steps(3))
    arrive(swap)
    for copy in everything:
        copy.wait_send()


def gather_copies(grid, chunk_count):
    high, low, depth, pair = grid.sizes
    first = lambda k: low - 1 if k % 2 == 0 else high - 1
    second = lambda k: high - 1 if k % 2 == 0 else low - 1
    return sum(
        (depth - 1) + first(k) + second(k) + (pair - 1) * (1 + first(k) + second(k))
        for k in range(chunk_count)
    )


def gather_all(grid, slab):
    rows = slab.shape[0]
    chunks = split_rows(rows, 4)
    copies = gather_copies(grid, len(chunks))
    return pl.pallas_call(
        partial(gather_kernel, grid, chunks),
        out_shape=jax.ShapeDtypeStruct(grid.sizes + slab.shape, slab.dtype),
        in_specs=[pl.BlockSpec(memory_space=pltpu.VMEM)],
        out_specs=pl.BlockSpec(memory_space=pltpu.VMEM),
        scratch_shapes=[
            pltpu.SemaphoreType.DMA((copies,)),
            pltpu.SemaphoreType.DMA((copies,)),
            pltpu.SemaphoreType.DMA,
        ],
        compiler_params=pltpu.CompilerParams(
            collective_id=0, has_side_effects=True, vmem_limit_bytes=48 * 1024 * 1024
        ),
    )(slab)


def scatter_kernel(grid, chunks, arrays, *refs):
    g_refs, refs = refs[:arrays], refs[arrays:]
    out_refs, refs = refs[:arrays], refs[arrays:]
    pair_bufs, refs = refs[:arrays], refs[arrays:]
    accs, refs = refs[:arrays], refs[arrays:]
    one_bufs, refs = refs[:arrays], refs[arrays:]
    two_bufs, refs = refs[:arrays], refs[arrays:]
    z_bufs, (send_sem, recv_sem) = refs[:arrays], refs[arrays:]
    here = grid.here()
    hi, lo, z, c = here
    spare = iter(range(send_sem.shape[0]))
    grid.barrier(here)
    everything = []

    def push(src, dst, spot):
        k = next(spare)
        copy = pltpu.make_async_remote_copy(
            src_ref=src, dst_ref=dst, send_sem=send_sem.at[k], recv_sem=recv_sem.at[k],
            device_id=grid.ident(spot), device_id_type=MESH,
        )
        copy.start()
        everything.append(copy)
        return copy

    def steps(axis):
        return [(s - 1, grid.peer(here, axis, s)) for s in range(1, grid.sizes[axis])]

    def arrive(copies):
        for copy in copies:
            copy.wait_recv()

    def add(into, terms, first, second):
        def body(t, _):
            i, j = t // second, t % second
            total = terms[0](i, j)[...].astype(jnp.float32)
            for term in terms[1:]:
                total = total + term(i, j)[...].astype(jnp.float32)
            target = into(i, j)
            target[...] = total.astype(target.dtype)
            return 0

        lax.fori_loop(0, first * second, body, 0)

    high, low, depth, pair = grid.sizes
    swaps, ones, twos, lines = [], [], [], []
    for n, start, size in chunks:
        rows = pl.ds(start, size)
        g_ref, pair_buf = g_refs[n], pair_bufs[n]
        swaps.append(
            [push(g_ref.at[:, :, :, spot[3], rows], pair_buf.at[:, :, :, rows], spot) for _, spot in steps(3)]
        )
    for k, (n, start, size) in enumerate(chunks):
        rows = pl.ds(start, size)
        g_ref, pair_buf, acc, buf_one = g_refs[n], pair_bufs[n], accs[n], one_bufs[n]
        arrive(swaps[k])
        terms = [lambda i, j: g_ref.at[i // low, i % low, j, c, rows]]
        if pair > 1:
            terms.append(lambda i, j: pair_buf.at[i // low, i % low, j, rows])
        add(lambda i, j: acc.at[i // low, i % low, j, rows], terms, high * low, depth)
        if k % 2 == 0:
            ones.append(
                [push(acc.at[spot[0], :, :, rows], buf_one.at[s, 0:low, :, rows], spot) for s, spot in steps(0)]
            )
        else:
            ones.append(
                [push(acc.at[:, spot[1], :, rows], buf_one.at[s, 0:high, :, rows], spot) for s, spot in steps(1)]
            )
    for k, (n, start, size) in enumerate(chunks):
        rows = pl.ds(start, size)
        acc, buf_one, buf_two = accs[n], one_bufs[n], two_bufs[n]
        arrive(ones[k])
        even = k % 2 == 0
        mine = (lambda i, j: acc.at[hi, i, j, rows]) if even else (lambda i, j: acc.at[i, lo, j, rows])
        terms = [mine] + [
            (lambda i, j, s=s: buf_one.at[s, i, j, rows]) for s, _ in steps(0 if even else 1)
        ]
        add(mine, terms, low if even else high, depth)
        if even:
            twos.append(
                [push(acc.at[hi, spot[1], :, rows], buf_two.at[s, :, rows], spot) for s, spot in steps(1)]
            )
        else:
            twos.append(
                [push(acc.at[spot[0], lo, :, rows], buf_two.at[s, :, rows], spot) for s, spot in steps(0)]
            )
    for k, (n, start, size) in enumerate(chunks):
        rows = pl.ds(start, size)
        acc, buf_two, buf_z = accs[n], two_bufs[n], z_bufs[n]
        arrive(twos[k])
        mine = lambda i, j: acc.at[hi, lo, j, rows]
        terms = [mine] + [
            (lambda i, j, s=s: buf_two.at[s, j, rows]) for s, _ in steps(1 if k % 2 == 0 else 0)
        ]
        add(mine, terms, 1, depth)
        lines.append(
            [push(acc.at[hi, lo, spot[2], rows], buf_z.at[s, rows], spot) for s, spot in steps(2)]
        )
    for k, (n, start, size) in enumerate(chunks):
        rows = pl.ds(start, size)
        acc, buf_z = accs[n], z_bufs[n]
        arrive(lines[k])
        total = acc[hi, lo, z, rows].astype(jnp.float32)
        for s in range(depth - 1):
            total = total + buf_z[s, rows].astype(jnp.float32)
        out_refs[n][rows, :] = total
    for copy in everything:
        copy.wait_send()


def scatter_sum(grid, arrays):
    high, low, depth, pair = grid.sizes
    chunks = []
    for n, array in enumerate(arrays):
        rows = array.shape[-2]
        if rows % (2 * SUBLANES) == 0:
            chunks += [(n, 0, rows // 2), (n, rows // 2, rows // 2)]
        else:
            chunks.append((n, 0, rows))
    copies = len(chunks) * (high + low + depth + pair - 4)
    kind = arrays[0].dtype
    tails = [array.shape[-2:] for array in arrays]
    side = max(high, low)
    shapes = [
        (high, low, depth), (high, low, depth), (max(side - 1, 1), side, depth),
        (max(side - 1, 1), depth), (max(depth - 1, 1),),
    ]
    return pl.pallas_call(
        partial(scatter_kernel, grid, chunks, len(arrays)),
        out_shape=[jax.ShapeDtypeStruct(tail, jnp.float32) for tail in tails],
        in_specs=[pl.BlockSpec(memory_space=pltpu.VMEM)] * len(arrays),
        out_specs=[pl.BlockSpec(memory_space=pltpu.VMEM)] * len(arrays),
        scratch_shapes=[pltpu.VMEM(shape + tail, kind) for shape in shapes for tail in tails]
        + [pltpu.SemaphoreType.DMA((copies,)), pltpu.SemaphoreType.DMA((copies,))],
        compiler_params=pltpu.CompilerParams(
            collective_id=1, has_side_effects=True, vmem_limit_bytes=48 * 1024 * 1024
        ),
    )(*arrays)


def padded_rows(extent):
    return -(-extent // LANES)


def pack(pieces, lead):
    parts = []
    for piece in pieces:
        extent = piece.shape[-1]
        rows = padded_rows(extent)
        gap = rows * LANES - extent
        if gap:
            piece = jnp.pad(piece, [(0, 0)] * len(lead) + [(0, gap)])
        parts.append(piece.reshape(lead + (rows, LANES)))
    total = sum(part.shape[-2] for part in parts)
    gap = -total % SUBLANES
    if gap:
        parts.append(jnp.zeros(lead + (gap, LANES), parts[0].dtype))
    return jnp.concatenate(parts, axis=-2)


def dot(left, right, contract=(1, 0)):
    return lax.dot_general(
        left, right, (((contract[0],), (contract[1],)), ((), ())), preferred_element_type=jnp.float32
    )


def block_kernel(
    count_ref, x_ref, cond_ref, cot_ref, w_ada, w_qkv, w_proj, w_one, w_two, bias_ref,
    out_ref, gx_ref, gcond_ref, g_ada, g_qkv, g_proj, g_one, g_two, gbias_ref,
    mod, norm_one, inv_one, h_one, qkv, probs, mixed, branch, norm_two, inv_two, h_two,
    pre, act, mlp, wide, back, dx, small, dqkv, dmod,
):
    slots, length, width = x_ref.shape
    hidden = w_one.shape[1]
    rows_all = slots * length
    heads = probs.shape[1]
    head_dim = width // heads
    score_scale = head_dim ** (-0.5)
    f32, b16 = jnp.float32, jnp.bfloat16
    tile = 256 if hidden % 256 == 0 else hidden
    count = count_ref[0]
    o_query, o_value = 6 * width, 7 * width
    o_proj, o_one, o_two = 8 * width, 9 * width, 9 * width + hidden
    lane = lax.broadcasted_iota(jnp.int32, (length, 2 * head_dim), 1)
    lower = lane < head_dim

    def slot_loop(body):
        def step(s, _):
            body(s, pl.ds(pl.multiple_of(s * length, length), length))
            return 0

        lax.fori_loop(0, slots, step, 0)

    def part(s, k):
        return mod[pl.ds(s, 1), k * width : (k + 1) * width]

    def only(pair_block, first):
        return jnp.where(lower if first else jnp.logical_not(lower), pair_block, jnp.zeros_like(pair_block))

    def column_sum(values):
        return jnp.sum(values, axis=0, keepdims=True)

    cond = cond_ref[...]
    cond_act = (cond * jax.nn.sigmoid(cond)).astype(b16)
    mod[...] = dot(cond_act, w_ada[...]) + bias_ref[:, : 6 * width]

    def norm_first(s, rows):
        normed, inverse = layer_norm(x_ref[s])
        norm_one[rows, :] = normed
        inv_one[rows, :] = inverse
        h_one[rows, :] = (normed * (1.0 + part(s, 1)) + part(s, 0)).astype(b16)

    slot_loop(norm_first)
    for k, offset in enumerate((o_query, None, o_value)):
        cols = slice(k * width, (k + 1) * width)
        value = dot(h_one[...], w_qkv[:, cols])
        if offset is not None:
            value = value + bias_ref[:, offset : offset + width]
        qkv[:, cols] = value.astype(b16)

    def attend(s, rows):
        for pair in range(heads // 2):
            at = pair * 2 * head_dim
            query = qkv[rows, at : at + 2 * head_dim]
            key = qkv[rows, width + at : width + at + 2 * head_dim]
            value = qkv[rows, 2 * width + at : 2 * width + at + 2 * head_dim]
            halves = []
            for h in range(2):
                scores = dot(only(query, h == 0), key, (1, 1)) * score_scale
                total = jnp.log(jnp.sum(jnp.exp(scores), axis=-1, keepdims=True))
                prob = jnp.exp(scores - total)
                probs[s, 2 * pair + h] = prob
                halves.append(dot(prob.astype(b16), value))
            mixed[rows, at : at + 2 * head_dim] = jnp.where(lower, halves[0], halves[1]).astype(b16)

    slot_loop(attend)
    branch[...] = dot(mixed[...], w_proj[...]) + bias_ref[:, o_proj : o_proj + width]

    def norm_second(s, rows):
        after = x_ref[s] + part(s, 2) * branch[rows, :]
        dx[rows, :] = after
        normed, inverse = layer_norm(after)
        norm_two[rows, :] = normed
        inv_two[rows, :] = inverse
        h_two[rows, :] = (normed * (1.0 + part(s, 4)) + part(s, 3)).astype(b16)

    slot_loop(norm_second)

    def up(t, _):
        cols = pl.ds(pl.multiple_of(t * tile, tile), tile)
        shift = bias_ref[:, pl.ds(pl.multiple_of(o_one + t * tile, LANES), tile)]
        value = dot(h_two[...], w_one[:, cols]) + shift
        pre[:, cols] = value
        act[:, cols] = gelu_value(value).astype(b16)
        return 0

    lax.fori_loop(0, hidden // tile, up, 0)
    mlp[...] = dot(act[...], w_two[...]) + bias_ref[:, o_two : o_two + width]

    gbias_ref[...] = jnp.zeros_like(gbias_ref)

    def finish(s, rows):
        live = s < count
        value = mlp[rows, :]
        out_ref[s] = jnp.where(live, dx[rows, :] + part(s, 5) * value, 0.0)
        grad = jnp.where(live, cot_ref[s], 0.0)
        dmod[pl.ds(s, 1), 5 * width :] = column_sum(grad * value)
        full = grad * part(s, 5)
        gbias_ref[:, o_two : o_two + width] += column_sum(full)
        small[rows, :] = full.astype(b16)

    slot_loop(finish)

    def down(t, _):
        cols = pl.ds(pl.multiple_of(t * tile, tile), tile)
        full = dot(small[...], w_two[cols, :], (1, 1)) * gelu_slope(pre[:, cols])
        gbias_ref[:, pl.ds(pl.multiple_of(o_one + t * tile, LANES), tile)] = column_sum(full)
        grad = full.astype(b16)
        wide[:, cols] = grad
        g_two[cols, :] = dot(act[:, cols], small[...], (0, 0)).astype(g_two.dtype)
        g_one[:, cols] = dot(h_two[...], grad, (0, 0)).astype(g_one.dtype)
        return 0

    lax.fori_loop(0, hidden // tile, down, 0)
    back[...] = dot(wide[...], w_one[...], (1, 1))

    def mlp_back(s, rows):
        grad_two = back[rows, :]
        normed = norm_two[rows, :]
        dmod[pl.ds(s, 1), 4 * width : 5 * width] = column_sum(grad_two * normed)
        dmod[pl.ds(s, 1), 3 * width : 4 * width] = column_sum(grad_two)
        after = jnp.where(s < count, cot_ref[s], 0.0) + norm_backward(
            grad_two * (1.0 + part(s, 4)), normed, inv_two[rows, :]
        )
        dx[rows, :] = after
        dmod[pl.ds(s, 1), 2 * width : 3 * width] = column_sum(after * branch[rows, :])
        full = after * part(s, 2)
        gbias_ref[:, o_proj : o_proj + width] += column_sum(full)
        small[rows, :] = full.astype(b16)

    slot_loop(mlp_back)
    g_proj[...] = dot(mixed[...], small[...], (0, 0)).astype(g_proj.dtype)
    mixed[...] = dot(small[...], w_proj[...], (1, 1)).astype(b16)

    def attend_back(s, rows):
        for pair in range(heads // 2):
            at = pair * 2 * head_dim
            span = slice(at, at + 2 * head_dim)
            query = qkv[rows, span]
            key = qkv[rows, width + at : width + at + 2 * head_dim]
            value = qkv[rows, 2 * width + at : 2 * width + at + 2 * head_dim]
            grad = mixed[rows, span]
            d_query, d_key, d_value = [], [], []
            for h in range(2):
                prob = probs[s, 2 * pair + h]
                d_prob = dot(only(grad, h == 0), value, (1, 1))
                d_value.append(dot(prob.astype(b16), grad, (0, 0)))
                delta = jnp.sum(prob * d_prob, axis=-1, keepdims=True)
                d_score = (prob * (d_prob - delta) * score_scale).astype(b16)
                d_query.append(dot(d_score, key))
                d_key.append(dot(d_score, query, (0, 0)))
            d_query = jnp.where(lower, d_query[0], d_query[1]).astype(b16)
            d_key = jnp.where(lower, d_key[0], d_key[1]).astype(b16)
            d_value = jnp.where(lower, d_value[0], d_value[1]).astype(b16)
            dqkv[rows, span] = d_query
            dqkv[rows, width + at : width + at + 2 * head_dim] = d_key
            dqkv[rows, 2 * width + at : 2 * width + at + 2 * head_dim] = d_value
            gbias_ref[:, o_query + at : o_query + at + 2 * head_dim] += column_sum(d_query.astype(f32))
            gbias_ref[:, o_value + at : o_value + at + 2 * head_dim] += column_sum(d_value.astype(f32))

    slot_loop(attend_back)
    for k in range(3):
        cols = slice(k * width, (k + 1) * width)
        g_qkv[:, cols] = dot(h_one[...], dqkv[:, cols], (0, 0)).astype(g_qkv.dtype)
    back[...] = dot(dqkv[...], w_qkv[...], (1, 1))

    def attn_back(s, rows):
        grad_one = back[rows, :]
        normed = norm_one[rows, :]
        dmod[pl.ds(s, 1), width : 2 * width] = column_sum(grad_one * normed)
        dmod[pl.ds(s, 1), :width] = column_sum(grad_one)
        gx_ref[s] = dx[rows, :] + norm_backward(
            grad_one * (1.0 + part(s, 1)), normed, inv_one[rows, :]
        )

    slot_loop(attn_back)
    gbias_ref[:, : 6 * width] = column_sum(dmod[...])
    grad_mod = dmod[...].astype(b16)
    g_ada[...] = dot(cond_act, grad_mod, (0, 0)).astype(g_ada.dtype)
    gcond_ref[...] = dot(grad_mod, w_ada[...], (1, 1)) * silu_slope(cond)


def run_block(counts, latents, conditioning, cotangent, weights, biases):
    slots, length, width = latents.shape
    w_ada, w_qkv, w_proj, w_one, w_two = weights
    hidden = w_one.shape[1]
    rows = slots * length
    f32, b16 = jnp.float32, jnp.bfloat16
    outs = [
        (latents.shape, f32), (latents.shape, f32), (conditioning.shape, f32),
        (w_ada.shape, b16), (w_qkv.shape, b16), (w_proj.shape, b16), (w_one.shape, b16),
        (w_two.shape, b16), (biases.shape, f32),
    ]
    scratch = [
        ((slots, 6 * width), f32), ((rows, width), f32), ((rows, 1), f32), ((rows, width), b16),
        ((rows, 3 * width), b16), ((slots, HEADS, length, length), f32), ((rows, width), b16),
        ((rows, width), f32), ((rows, width), f32), ((rows, 1), f32), ((rows, width), b16),
        ((rows, hidden), f32), ((rows, hidden), b16), ((rows, width), f32), ((rows, hidden), b16),
        ((rows, width), f32), ((rows, width), f32), ((rows, width), b16), ((rows, 3 * width), b16),
        ((slots, 6 * width), f32),
    ]
    vmem = pl.BlockSpec(memory_space=pltpu.VMEM)
    return pl.pallas_call(
        block_kernel,
        out_shape=[jax.ShapeDtypeStruct(shape, kind) for shape, kind in outs],
        in_specs=[pl.BlockSpec(memory_space=pltpu.SMEM)] + [vmem] * 9,
        out_specs=[vmem] * len(outs),
        scratch_shapes=[pltpu.VMEM(shape, kind) for shape, kind in scratch],
        compiler_params=pltpu.CompilerParams(vmem_limit_bytes=60 * 1024 * 1024),
    )(counts, latents, conditioning, cotangent, *weights, biases)


def local(
    grid, latents, conditioning, counts, cotangent, ada_weights, attn_weights, mlp_weights, flat_biases
):
    model_width = latents.shape[-1]
    shards = (ada_weights, attn_weights, mlp_weights, flat_biases)
    gathered = gather_all(grid, pack(shards, ()))
    gathered = gathered.reshape((grid.count,) + gathered.shape[-2:])
    flats, row = [], 0
    for shard in shards:
        extent = shard.shape[0]
        rows = padded_rows(extent)
        flats.append(
            gathered[:, row : row + rows].reshape(grid.count, rows * LANES)[:, :extent].reshape(-1)
        )
        row += rows
    weights = unpack(flats[0], flats[1], flats[2], flats[3], model_width, FF)[:5]
    biases = flats[3].astype(jnp.float32)[None]
    output, grad_latents, grad_conditioning, g_ada, g_qkv, g_proj, g_one, g_two, g_bias = run_block(
        counts, latents, conditioning, cotangent, weights, biases
    )

    def lines(flat, extent):
        rows = padded_rows(extent)
        flat = flat.reshape(grid.count, extent)
        if rows * LANES != extent:
            flat = jnp.pad(flat, ((0, 0), (0, rows * LANES - extent)))
        return flat.reshape(grid.sizes + (rows, LANES))

    flat_grads = [
        g_ada.reshape(-1),
        jnp.concatenate([g_qkv.reshape(-1), g_proj.reshape(-1)]),
        jnp.concatenate([g_one.reshape(-1), g_two.reshape(-1)]),
        g_bias.astype(jnp.bfloat16).reshape(-1),
    ]
    sums = scatter_sum(grid, [lines(flat, shard.shape[0]) for flat, shard in zip(flat_grads, shards)])
    grads = tuple(total.reshape(-1)[: shard.shape[0]] for total, shard in zip(sums, shards))
    return (output, grad_latents, grad_conditioning) + grads


def solution(mesh):
    in_specs = (
        P(("dp", "fsdp"), None, None),
        P(("dp", "fsdp"), None),
        P(("dp", "fsdp")),
        P(("dp", "fsdp"), None, None),
        P(("dp", "fsdp")),
        P(("dp", "fsdp")),
        P(("dp", "fsdp")),
        P(("dp", "fsdp")),
    )
    out_specs = (
        P(("dp", "fsdp"), None, None),
        P(("dp", "fsdp"), None, None),
        P(("dp", "fsdp"), None),
        P(("dp", "fsdp")),
        P(("dp", "fsdp")),
        P(("dp", "fsdp")),
        P(("dp", "fsdp")),
    )
    return jax.shard_map(partial(local, Grid(mesh)), mesh=mesh, in_specs=in_specs, out_specs=out_specs, check_vma=False)
```

time: 253 us -> 167 us (0.66)
  local copies, waits for them, and re-layouts: 98 us -> 40.7 us
  matrix products: 51.3 us -> 0 us
  Pallas kernels: 85.1 us -> 122 us
  other arithmetic: 14.6 us -> 2.72 us
    dot_general x21 -> x0, matrix products: 51.3 us -> none  [the longest x15 31.8 us: mat_dot(): return jnp.dot(left, right, preferred_element_type=jnp.float32)]
    pallas_call x1 -> x2, Pallas kernels: 43.6 us -> 80 us  [the longest x1 43.5 us: scatter_sum(): pl.pallas_call(partial(scatter_kernel, grid, chunks, len(arrays)), out_sh...]
    concatenate x4 -> x1, local copies, waits for them, and re-layouts: 27 us -> 2.52 us  [pack(): return jnp.concatenate(parts, axis=-2)]
    unnamed x74 -> x13, local copies, waits for them, and re-layouts: 16.9 us -> 7.52 us
    concatenate x7 -> x2, local copies, waits for them, and re-layouts: 10.8 us -> 3.58 us  [local(): jnp.concatenate([g_one.reshape(-1), g_two.reshape(-1)])]
    reduce_sum x7 -> x0, other arithmetic: 6.94 us -> none  [the longest x1 3.61 us: forward_group(): log_total = jnp.log(jnp.sum(jnp.exp(scores), axis=-1, keepdims=True))]
    reshape x2 -> x1, local copies, waits for them, and re-layouts: 6.93 us -> 2.16 us  [unpack(): mlp_flat[:fc1_size].reshape(model_width, hidden_units)]
    convert_element_type x7 -> x1, local copies, waits for them, and re-layouts: 5.27 us -> 0.73 us  [local(): biases = flats[3].astype(jnp.float32)[None]]
where the time goes in v2:
time: 167 us; the launch traced here: 166 us
  Pallas kernels  122 us (73%)
  local copies, waits for them, and re-layouts  40.7 us (24%)
  other arithmetic  2.72 us (2%)
    pallas_call x1, Pallas kernels, scatter_sum(): pl.pallas_call(partial(scatter_kernel, grid, chunks, len(arrays)), out_sh...  43.5 us
    pallas_call x1, Pallas kernels, gather_all(): pl.pallas_call(partial(gather_kernel, grid, chunks), out_shape=jax.ShapeD...  41.5 us
    pallas_call x1, Pallas kernels, run_block(): pl.pallas_call(block_kernel, out_shape=[jax.ShapeDtypeStruct(shape, kind)...  36.5 us
    unnamed x13, local copies, waits for them, and re-layouts  7.52 us
    another operation x1, local copies, waits for them, and re-layouts, lines(): return flat.reshape(grid.sizes + (rows, LANES))  4.5 us
    concatenate x2, local copies, waits for them, and re-layouts, local(): jnp.concatenate([g_one.reshape(-1), g_two.reshape(-1)])  3.58 us

profile of v2, /device:TPU:0, one launch (start us, length us, event | category | flops | bytes accessed | tf_op | source)
XLA Modules:
  0.0 166.3 jit_solution(12873470150925117097)
XLA Ops:
  1.9 2.5 %concatenate.14.in_ref = bf16[656,128]{1,0:T(8,128)(2,1)S(1)} concatenate(bf16[216,128]{1,0:T(8,128)(2,1)} %bitcast.29, bf16[144,128]{1,0:T(8,128)(2,1)} %bitcast.30, bf16[288,128]{1,0:T(8,128)(2,1)} %bitcast.26, bf16[2,128]{1,0:T(2,128)(2,1)S(1)} %pad_bitcast_fusion, bf16[6,128]{1,0:T(8,128)(2,1)S(1)} %broadcast_in_dim.4), dimensions={0} | concatenate | bytes 335872 | tf_op jit(solution)/shard_map/concatenate | solution.py:376
  4.5 41.5 %shard_map.135 = bf16[2,2,4,2,656,128]{5,4,3,2,1,0:T(8,128)(2,1)S(1)} custom-call(bf16[656,128]{1,0:T(8,128)(2,1)S(1)} %concatenate.14.in_ref), custom_call_target="tpu_custom_call" | custom-call | tf_op jit(solution)/shard_map/pallas_call | solution.py:204
  46.0 2.3 %copy-done = bf16[2,2,4,2,656,128]{5,4,3,2,1,0:T(8,128)(2,1)} copy-done((bf16[2,2,4,2,656,128]{5,4,3,2,1,0:T(8,128)(2,1)}, bf16[2,2,4,2,656,128]{5,4,3,2,1,0:T(8,128)(2,1)S(1)}, u32[]{:S(2)}) %copy-start) | copy-done | bytes 5373976
  48.4 0.7 reshape.109.bias_ref
  49.1 1.0 slice.44
  50.1 0.8 reshape.98.w_proj
  50.9 1.2 slice.43
  52.2 2.0 %reshape.97.w_qkv = bf16[384,1152]{1,0:T(8,128)(2,1)} reshape(bf16[24,144,128]{2,1,0:T(8,128)(2,1)S(1)} %slice.43) | data formatting | bytes 1769472 | tf_op jit(solution)/shard_map/reshape | solution.py:54
  54.1 1.6 slice.42
  55.7 2.8 %fusion = (bf16[16,288,128]{2,1,0:T(8,128)(2,1)}, bf16[16,288,128]{2,1,0:T(8,128)(2,1)S(1)}) fusion(bf16[32,656,128]{2,1,0:T(8,128)(2,1)} %bitcast.20), kind=kLoop, calls=%fused_computation.6 | loop fusion | bytes 4718592 | tf_op jit(solution)/shard_map/slice | solution.py:57
  58.6 3.1 %reshape.100.w_two = bf16[1536,384]{1,0:T(8,128)(2,1)} reshape(bf16[16,288,128]{2,1,0:T(8,128)(2,1)} %get-tuple-element.33) | data formatting | bytes 2359296 | tf_op jit(solution)/shard_map/reshape | solution.py:57
  61.7 3.0 %reshape_reshape_reshape.6.w_ada = bf16[384,2304]{1,0:T(8,128)(2,1)} reshape(bf16[32,216,128]{2,1,0:T(8,128)(2,1)S(1)} %slice.42) | data formatting | bytes 3538944 | tf_op jit(solution)/shard_map/reshape;reshape;reshape | solution.py:53
  64.7 2.2 %reshape.99.w_one = bf16[384,1536]{1,0:T(8,128)(2,1)} reshape(bf16[16,288,128]{2,1,0:T(8,128)(2,1)S(1)} %get-tuple-element.34) | data formatting | bytes 2359296 | tf_op jit(solution)/shard_map/reshape | solution.py:56
  66.8 36.5 %shard_map.136 = (f32[4,128,384]{2,1,0:T(8,128)}, f32[4,128,384]{2,1,0:T(8,128)}, f32[4,384]{1,0:T(4,128)}, bf16[384,2304]{1,0:T(8,128)(2,1)}, bf16[384,1152]{1,...) custom-call(s32[1]{0:T(128)S(6)} %copy.22.count_ref, ...), custom_call_target="tpu_custom_call" | custom-call | tf_op jit(solution)/shard_map/pallas_call | solution.py:591
  103.3 0.8 convert_reduce_fusion
  104.3 1.1 reshape.103
  105.4 2.2 %reshape.102 = bf16[442368]{0:T(1024)(128)(2,1)S(1)} reshape(bf16[384,1152]{1,0:T(8,128)(2,1)} %get-tuple-element.24) | data formatting | bytes 1769472 | tf_op jit(solution)/shard_map/reshape | solution.py:631
  107.7 1.2 copy-done.3
  108.9 2.2 %concatenate.16 = bf16[1,2,4,2,288,128]{5,4,3,2,1,0:T(8,128)(2,1)} reshape(bf16[384,1536]{1,0:T(8,128)(2,1)S(1)} %copy-done.3) | data formatting | bytes 2359296 | tf_op jit(solution)/shard_map/concatenate | solution.py:632
  111.1 1.4 concatenate.17
  112.5 1.8 %pad_maximum_fusion.refs_2_ = bf16[2,2,4,2,288,128]{5,4,3,2,1,0:T(8,128)(2,1)S(1)} fusion(bf16[1,2,4,2,288,128]{5,4,3,2,1,0:T(8,128)(2,1)} %concatenate.17, bf16[1,2,4,2,288,128]{5,4,3,2,1,0:T(8,128)(2,1)} %concatenate.16), kind=kLoop, calls=%fused_computation | loop fusion | flops 1179648 | bytes 4718592 | tf_op jit(solution)/shard_map/concatenate | solution.py:632
  114.3 4.5 %reshape_reshape_reshape.7.refs_0_ = bf16[2,2,4,2,216,128]{5,4,3,2,1,0:T(8,128)(2,1)} reshape(bf16[384,2304]{1,0:T(8,128)(2,1)} %get-tuple-element.23) | data formatting | bytes 3538944 | tf_op jit(solution)/shard_map/reshape;reshape;reshape | solution.py:627
  118.8 1.5 copy-done.1
  120.3 43.5 %shard_map.137 = (f32[216,128]{1,0:T(8,128)S(1)}, f32[144,128]{1,0:T(8,128)S(1)}, f32[288,128]{1,0:T(8,128)S(1)}, f32[2,128]{1,0:T(2,128)S(1)}) custom-call(bf16[2,2,4,2,216,128]{5,4,3,2,1,0:T(8,128)(2,1)S(1)} %copy-done.1, bf16[2,2,4,2,144,128]{5,4,3,2,1,0:T(8,128)(2,1)S(1)} %bitcast.21, bf16[2,2,4,2,288,128]{5,4,3,2,1,0:T(8,128)(2,1)S(1)} %pad_maximum_fusion.refs_2_, ...), custom_call_target="tpu_custom_call" | custom-call | tf_op jit(solution)/shard_map/pallas_call | solution.py:346
  (18 shorter events, 3.4 us)
Async XLA Ops:
  46.0 2.3 %copy-start = (bf16[2,2,4,2,656,128]{5,4,3,2,1,0:T(8,128)(2,1)}, bf16[2,2,4,2,656,128]{5,4,3,2,1,0:T(8,128)(2,1)S(1)}, u32[]{:S(2)}) copy-start(bf16[2,2,4,2,656,128]{5,4,3,2,1,0:T(8,128)(2,1)S(1)} %shard_map.135) | copy-start | bytes 16121860
  107.6 1.3 copy-start.3
  108.9 2.2 %copy-start.2 = (bf16[1536,384]{1,0:T(8,128)(2,1)S(1)}, bf16[1536,384]{1,0:T(8,128)(2,1)}, u32[]{:S(2)}) copy-start(bf16[1536,384]{1,0:T(8,128)(2,1)} %get-tuple-element.27) | copy-start | bytes 3538948
  118.8 1.5 copy-start.1

commit v3 on v2

--- a/solution.py
+++ b/solution.py
@@ -111,142 +111,171 @@
         pl.semaphore_wait(sem, total)
 
 
-def split_rows(rows, parts):
-    units = rows // SUBLANES
-    parts = min(parts, units)
-    cuts = [units * k // parts for k in range(parts + 1)]
-    return [(cuts[k] * SUBLANES, (cuts[k + 1] - cuts[k]) * SUBLANES) for k in range(parts)]
-
-
-def gather_kernel(grid, chunks, in_ref, out_ref, send_sem, recv_sem, own_sem):
-    here = grid.here()
-    hi, lo, z, c = here
-    spare = iter(range(send_sem.shape[0]))
-    grid.barrier(here)
-
-    def push(src, dst, spot):
-        k = next(spare)
+def chunk_rows(arrays):
+    chunks = []
+    for n, array in enumerate(arrays):
+        rows = array.shape[-2]
+        if rows % (2 * SUBLANES) == 0:
+            chunks += [(n, 0, rows // 2), (n, rows // 2, rows // 2)]
+        else:
+            chunks.append((n, 0, rows))
+    return chunks
+
+
+class Mover:
+    def __init__(self, grid, send_sem, recv_sem):
+        self.grid, self.here = grid, grid.here()
+        self.send_sem, self.recv_sem = send_sem, recv_sem
+        self.started = []
+
+    def push(self, src, dst, spot):
+        k = len(self.started)
         copy = pltpu.make_async_remote_copy(
-            src_ref=src, dst_ref=dst, send_sem=send_sem.at[k], recv_sem=recv_sem.at[k],
-            device_id=grid.ident(spot), device_id_type=MESH,
+            src_ref=src, dst_ref=dst, send_sem=self.send_sem.at[k], recv_sem=self.recv_sem.at[k],
+            device_id=self.grid.ident(spot), device_id_type=MESH,
         )
         copy.start()
+        self.started.append(copy)
         return copy
 
-    def steps(axis):
-        return [grid.peer(here, axis, s) for s in range(1, grid.sizes[axis])]
-
-    everything = []
-
-    def pushes(src, dst, spots):
-        copies = [push(src, dst, spot) for spot in spots]
-        everything.extend(copies)
-        return copies
-
-    def arrive(copies):
-        for copy in copies:
-            copy.wait_recv()
-
-    own = pltpu.make_async_copy(in_ref, out_ref.at[hi, lo, z, c], own_sem)
-    own.start()
-    along_z, first, second, swap = [], [], [], []
-    for start, size in chunks:
-        rows = pl.ds(start, size)
-        along_z.append(pushes(in_ref.at[rows], out_ref.at[hi, lo, z, c, rows], steps(2)))
-    own.wait()
-    for k, (start, size) in enumerate(chunks):
-        rows = pl.ds(start, size)
-        arrive(along_z[k])
-        part = out_ref.at[hi, lo, :, c, rows]
-        first.append(pushes(part, part, steps(1 if k % 2 == 0 else 0)))
-        swap += pushes(part, part, steps(3))
-    for k, (start, size) in enumerate(chunks):
-        rows = pl.ds(start, size)
-        arrive(first[k])
-        if k % 2 == 0:
-            part = out_ref.at[hi, :, :, c, rows]
-            second.append(pushes(part, part, steps(0)))
-            others = [out_ref.at[hi, spot[1], :, c, rows] for spot in steps(1)]
+    def spots(self, axis):
+        return [self.grid.peer(self.here, axis, s) for s in range(1, self.grid.sizes[axis])]
+
+    def pushes(self, ref, axis):
+        return [self.push(ref, ref, spot) for spot in self.spots(axis)]
+
+    def drain(self):
+        for copy in self.started:
+            copy.wait_send()
+
+
+def arrive(copies):
+    for copy in copies:
+        copy.wait_recv()
+
+
+class Spread:
+    def __init__(self, mover, in_ref, out_ref, rows, low_first):
+        self.mover, self.in_ref, self.out_ref, self.rows = mover, in_ref, out_ref, rows
+        self.low_first = low_first
+        self.swap = []
+
+    def begin(self):
+        hi, lo, z, c = self.mover.here
+        src, dst = self.in_ref.at[self.rows], self.out_ref.at[hi, lo, z, c, self.rows]
+        self.pending = [self.mover.push(src, dst, spot) for spot in self.mover.spots(2)]
+
+    def first(self):
+        hi, lo, z, c = self.mover.here
+        arrive(self.pending)
+        part = self.out_ref.at[hi, lo, :, c, self.rows]
+        self.pending = self.mover.pushes(part, 1 if self.low_first else 0)
+        self.swap += self.mover.pushes(part, 3)
+
+    def second(self):
+        hi, lo, z, c = self.mover.here
+        arrive(self.pending)
+        out, rows = self.out_ref, self.rows
+        if self.low_first:
+            self.pending = self.mover.pushes(out.at[hi, :, :, c, rows], 0)
+            others = [out.at[hi, spot[1], :, c, rows] for spot in self.mover.spots(1)]
         else:
-            part = out_ref.at[:, lo, :, c, rows]
-            second.append(pushes(part, part, steps(1)))
-            others = [out_ref.at[spot[0], lo, :, c, rows] for spot in steps(0)]
+            self.pending = self.mover.pushes(out.at[:, lo, :, c, rows], 1)
+            others = [out.at[spot[0], lo, :, c, rows] for spot in self.mover.spots(0)]
         for other in others:
-            swap += pushes(other, other, steps(3))
-    for k, (start, size) in enumerate(chunks):
-        rows = pl.ds(start, size)
-        arrive(second[k])
-        if k % 2 == 0:
-            others = [out_ref.at[spot[0], :, :, c, rows] for spot in steps(0)]
+            self.swap += self.mover.pushes(other, 3)
+
+    def third(self):
+        hi, lo, z, c = self.mover.here
+        arrive(self.pending)
+        out, rows = self.out_ref, self.rows
+        if self.low_first:
+            others = [out.at[spot[0], :, :, c, rows] for spot in self.mover.spots(0)]
         else:
-            others = [out_ref.at[:, spot[1], :, c, rows] for spot in steps(1)]
+            others = [out.at[:, spot[1], :, c, rows] for spot in self.mover.spots(1)]
         for other in others:
-            swap += pushes(other, other, steps(3))
-    arrive(swap)
-    for copy in everything:
-        copy.wait_send()
-
-
-def gather_copies(grid, chunk_count):
-    high, low, depth, pair = grid.sizes
-    first = lambda k: low - 1 if k % 2 == 0 else high - 1
-    second = lambda k: high - 1 if k % 2 == 0 else low - 1
-    return sum(
-        (depth - 1) + first(k) + second(k) + (pair - 1) * (1 + first(k) + second(k))
-        for k in range(chunk_count)
-    )
-
-
-def gather_all(grid, slab):
-    rows = slab.shape[0]
-    chunks = split_rows(rows, 4)
-    copies = gather_copies(grid, len(chunks))
+            self.swap += self.mover.pushes(other, 3)
+
+    def end(self):
+        arrive(self.swap)
+
+    @staticmethod
+    def copies(grid):
+        high, low, depth, pair = grid.sizes
+        return depth - 1 + (high + low - 2) + (pair - 1) * (1 + high + low - 2)
+
+
+def gather_kernel(grid, chunks, arrays, *refs):
+    in_refs, out_refs = refs[:arrays], refs[arrays : 2 * arrays]
+    send_sem, recv_sem, own_sem = refs[2 * arrays :]
+    mover = Mover(grid, send_sem, recv_sem)
+    hi, lo, z, c = mover.here
+    grid.barrier(mover.here)
+    own = [
+        pltpu.make_async_copy(in_refs[n], out_refs[n].at[hi, lo, z, c], own_sem.at[n])
+        for n in range(arrays)
+    ]
+    for copy in own:
+        copy.start()
+    spreads = [
+        Spread(mover, in_refs[n], out_refs[n], pl.ds(start, size), k % 2 == 0)
+        for k, (n, start, size) in enumerate(chunks)
+    ]
+    for spread in spreads:
+        spread.begin()
+    for copy in own:
+        copy.wait()
+    for spread in spreads:
+        spread.first()
+    for spread in spreads:
+        spread.second()
+    for spread in spreads:
+        spread.third()
+    for spread in spreads:
+        spread.end()
+    mover.drain()
+
+
+def gather_all(grid, arrays):
+    chunks = chunk_rows(arrays)
+    copies = Spread.copies(grid) * len(chunks)
+    vmem = pl.BlockSpec(memory_space=pltpu.VMEM)
     return pl.pallas_call(
-        partial(gather_kernel, grid, chunks),
-        out_shape=jax.ShapeDtypeStruct(grid.sizes + slab.shape, slab.dtype),
-        in_specs=[pl.BlockSpec(memory_space=pltpu.VMEM)],
-        out_specs=pl.BlockSpec(memory_space=pltpu.VMEM),
+        partial(gather_kernel, grid, chunks, len(arrays)),
+        out_shape=[jax.ShapeDtypeStruct(grid.sizes + array.shape, array.dtype) for array in arrays],
+        in_specs=[vmem] * len(arrays),
+        out_specs=[vmem] * len(arrays),
         scratch_shapes=[
             pltpu.SemaphoreType.DMA((copies,)),
             pltpu.SemaphoreType.DMA((copies,)),
-            pltpu.SemaphoreType.DMA,
+            pltpu.SemaphoreType.DMA((len(arrays),)),
         ],
         compiler_params=pltpu.CompilerParams(
             collective_id=0, has_side_effects=True, vmem_limit_bytes=48 * 1024 * 1024
         ),
-    )(slab)
-
-
-def scatter_kernel(grid, chunks, arrays, *refs):
+    )(*arrays)
+
+
+def scatter_kernel(grid, chunks, arrays, note_ref, *refs):
     g_refs, refs = refs[:arrays], refs[arrays:]
+    note_out, refs = refs[0], refs[1:]
     out_refs, refs = refs[:arrays], refs[arrays:]
     pair_bufs, refs = refs[:arrays], refs[arrays:]
     accs, refs = refs[:arrays], refs[arrays:]
     one_bufs, refs = refs[:arrays], refs[arrays:]
     two_bufs, refs = refs[:arrays], refs[arrays:]
-    z_bufs, (send_sem, recv_sem) = refs[:arrays], refs[arrays:]
-    here = grid.here()
+    z_bufs, (send_sem, recv_sem, own_sem) = refs[:arrays], refs[arrays:]
+    mover = Mover(grid, send_sem, recv_sem)
+    here, push = mover.here, mover.push
     hi, lo, z, c = here
-    spare = iter(range(send_sem.shape[0]))
     grid.barrier(here)
-    everything = []
-
-    def push(src, dst, spot):
-        k = next(spare)
-        copy = pltpu.make_async_remote_copy(
-            src_ref=src, dst_ref=dst, send_sem=send_sem.at[k], recv_sem=recv_sem.at[k],
-            device_id=grid.ident(spot), device_id_type=MESH,
-        )
-        copy.start()
-        everything.append(copy)
-        return copy
+    own = pltpu.make_async_copy(note_ref, note_out.at[hi, lo, z, c], own_sem)
+    own.start()
+    note = Spread(mover, note_ref, note_out, pl.ds(0, note_ref.shape[0]), True)
+    note.begin()
 
     def steps(axis):
         return [(s - 1, grid.peer(here, axis, s)) for s in range(1, grid.sizes[axis])]
-
-    def arrive(copies):
-        for copy in copies:
-            copy.wait_recv()
 
     def add(into, terms, first, second):
         def body(t, _):
@@ -268,6 +297,8 @@
         swaps.append(
             [push(g_ref.at[:, :, :, spot[3], rows], pair_buf.at[:, :, :, rows], spot) for _, spot in steps(3)]
         )
+    own.wait()
+    note.first()
     for k, (n, start, size) in enumerate(chunks):
         rows = pl.ds(start, size)
         g_ref, pair_buf, acc, buf_one = g_refs[n], pair_bufs[n], accs[n], one_bufs[n]
@@ -284,6 +315,7 @@
             ones.append(
                 [push(acc.at[:, spot[1], :, rows], buf_one.at[s, 0:high, :, rows], spot) for s, spot in steps(1)]
             )
+    note.second()
     for k, (n, start, size) in enumerate(chunks):
         rows = pl.ds(start, size)
         acc, buf_one, buf_two = accs[n], one_bufs[n], two_bufs[n]
@@ -302,6 +334,7 @@
             twos.append(
                 [push(acc.at[spot[0], lo, :, rows], buf_two.at[s, :, rows], spot) for s, spot in steps(0)]
             )
+    note.third()
     for k, (n, start, size) in enumerate(chunks):
         rows = pl.ds(start, size)
         acc, buf_two, buf_z = accs[n], two_bufs[n], z_bufs[n]
@@ -322,20 +355,14 @@
         for s in range(depth - 1):
             total = total + buf_z[s, rows].astype(jnp.float32)
         out_refs[n][rows, :] = total
-    for copy in everything:
-        copy.wait_send()
-
-
-def scatter_sum(grid, arrays):
+    note.end()
+    mover.drain()
+
+
+def scatter_sum(grid, arrays, note):
     high, low, depth, pair = grid.sizes
-    chunks = []
-    for n, array in enumerate(arrays):
-        rows = array.shape[-2]
-        if rows % (2 * SUBLANES) == 0:
-            chunks += [(n, 0, rows // 2), (n, rows // 2, rows // 2)]
-        else:
-            chunks.append((n, 0, rows))
-    copies = len(chunks) * (high + low + depth + pair - 4)
+    chunks = chunk_rows(arrays)
+    copies = len(chunks) * (high + low + depth + pair - 4) + Spread.copies(grid)
     kind = arrays[0].dtype
     tails = [array.shape[-2:] for array in arrays]
     side = max(high, low)
@@ -343,17 +370,19 @@
         (high, low, depth), (high, low, depth), (max(side - 1, 1), side, depth),
         (max(side - 1, 1), depth), (max(depth - 1, 1),),
     ]
+    vmem = pl.BlockSpec(memory_space=pltpu.VMEM)
     return pl.pallas_call(
         partial(scatter_kernel, grid, chunks, len(arrays)),
-        out_shape=[jax.ShapeDtypeStruct(tail, jnp.float32) for tail in tails],
-        in_specs=[pl.BlockSpec(memory_space=pltpu.VMEM)] * len(arrays),
-        out_specs=[pl.BlockSpec(memory_space=pltpu.VMEM)] * len(arrays),
+        out_shape=[jax.ShapeDtypeStruct(grid.sizes + note.shape, note.dtype)]
+        + [jax.ShapeDtypeStruct(tail, jnp.float32) for tail in tails],
+        in_specs=[vmem] * (1 + len(arrays)),
+        out_specs=[vmem] * (1 + len(arrays)),
         scratch_shapes=[pltpu.VMEM(shape + tail, kind) for shape in shapes for tail in tails]
-        + [pltpu.SemaphoreType.DMA((copies,)), pltpu.SemaphoreType.DMA((copies,))],
+        + [pltpu.SemaphoreType.DMA((copies,)), pltpu.SemaphoreType.DMA((copies,)), pltpu.SemaphoreType.DMA],
         compiler_params=pltpu.CompilerParams(
             collective_id=1, has_side_effects=True, vmem_limit_bytes=48 * 1024 * 1024
         ),
-    )(*arrays)
+    )(note, *arrays)
 
 
 def padded_rows(extent):
@@ -369,10 +398,8 @@
         if gap:
             piece = jnp.pad(piece, [(0, 0)] * len(lead) + [(0, gap)])
         parts.append(piece.reshape(lead + (rows, LANES)))
-    total = sum(part.shape[-2] for part in parts)
-    gap = -total % SUBLANES
-    if gap:
-        parts.append(jnp.zeros(lead + (gap, LANES), parts[0].dtype))
+    if len(parts) == 1:
+        return parts[0]
     return jnp.concatenate(parts, axis=-2)
 
 
@@ -384,7 +411,7 @@
 
 def block_kernel(
     count_ref, x_ref, cond_ref, cot_ref, w_ada, w_qkv, w_proj, w_one, w_two, bias_ref,
-    out_ref, gx_ref, gcond_ref, g_ada, g_qkv, g_proj, g_one, g_two, gbias_ref,
+    out_ref, gx_ref, gcond_ref, act_ref, dmod_ref, g_qkv, g_proj, g_one, g_two, gbias_ref,
     mod, norm_one, inv_one, h_one, qkv, probs, mixed, branch, norm_two, inv_two, h_two,
     pre, act, mlp, wide, back, dx, small, dqkv, dmod,
 ):
@@ -564,7 +591,8 @@
     slot_loop(attn_back)
     gbias_ref[:, : 6 * width] = column_sum(dmod[...])
     grad_mod = dmod[...].astype(b16)
-    g_ada[...] = dot(cond_act, grad_mod, (0, 0)).astype(g_ada.dtype)
+    act_ref[...] = cond_act
+    dmod_ref[...] = grad_mod
     gcond_ref[...] = dot(grad_mod, w_ada[...], (1, 1)) * silu_slope(cond)
 
 
@@ -576,7 +604,7 @@
     f32, b16 = jnp.float32, jnp.bfloat16
     outs = [
         (latents.shape, f32), (latents.shape, f32), (conditioning.shape, f32),
-        (w_ada.shape, b16), (w_qkv.shape, b16), (w_proj.shape, b16), (w_one.shape, b16),
+        (conditioning.shape, b16), ((slots, 6 * width), b16), (w_qkv.shape, b16), (w_proj.shape, b16), (w_one.shape, b16),
         (w_two.shape, b16), (biases.shape, f32),
     ]
     scratch = [
@@ -602,21 +630,16 @@
     grid, latents, conditioning, counts, cotangent, ada_weights, attn_weights, mlp_weights, flat_biases
 ):
     model_width = latents.shape[-1]
+    slots = latents.shape[0]
     shards = (ada_weights, attn_weights, mlp_weights, flat_biases)
-    gathered = gather_all(grid, pack(shards, ()))
-    gathered = gathered.reshape((grid.count,) + gathered.shape[-2:])
-    flats, row = [], 0
-    for shard in shards:
-        extent = shard.shape[0]
-        rows = padded_rows(extent)
-        flats.append(
-            gathered[:, row : row + rows].reshape(grid.count, rows * LANES)[:, :extent].reshape(-1)
-        )
-        row += rows
+    flats = [
+        whole.reshape(grid.count, -1)[:, : shard.shape[0]].reshape(-1)
+        for whole, shard in zip(gather_all(grid, [pack([shard], ()) for shard in shards]), shards)
+    ]
     weights = unpack(flats[0], flats[1], flats[2], flats[3], model_width, FF)[:5]
     biases = flats[3].astype(jnp.float32)[None]
-    output, grad_latents, grad_conditioning, g_ada, g_qkv, g_proj, g_one, g_two, g_bias = run_block(
-        counts, latents, conditioning, cotangent, weights, biases
+    output, grad_latents, grad_conditioning, cond_act, grad_mod, g_qkv, g_proj, g_one, g_two, g_bias = (
+        run_block(counts, latents, conditioning, cotangent, weights, biases)
     )
 
     def lines(flat, extent):
@@ -627,14 +650,33 @@
         return flat.reshape(grid.sizes + (rows, LANES))
 
     flat_grads = [
-        g_ada.reshape(-1),
         jnp.concatenate([g_qkv.reshape(-1), g_proj.reshape(-1)]),
         jnp.concatenate([g_one.reshape(-1), g_two.reshape(-1)]),
         g_bias.astype(jnp.bfloat16).reshape(-1),
     ]
-    sums = scatter_sum(grid, [lines(flat, shard.shape[0]) for flat, shard in zip(flat_grads, shards)])
-    grads = tuple(total.reshape(-1)[: shard.shape[0]] for total, shard in zip(sums, shards))
-    return (output, grad_latents, grad_conditioning) + grads
+    note = pack([grad_mod.reshape(-1), cond_act.reshape(-1)], ())
+    notes, *sums = scatter_sum(
+        grid, [lines(flat, shard.shape[0]) for flat, shard in zip(flat_grads, shards[1:])], note
+    )
+    notes = notes.reshape((grid.count,) + note.shape)
+    mod_rows, act_rows = grad_mod.size // LANES, cond_act.size // LANES
+    all_mod = notes[:, :mod_rows].reshape(grid.count * slots, 6 * model_width)
+    all_act = notes[:, mod_rows : mod_rows + act_rows].reshape(grid.count * slots, model_width)
+    grads = [own_rows(all_act, all_mod, ada_weights.shape[0])]
+    grads += [total.reshape(-1)[: shard.shape[0]] for total, shard in zip(sums, shards[1:])]
+    return (output, grad_latents, grad_conditioning) + tuple(grads)
+
+
+def own_rows(left, right, extent):
+    wide = right.shape[1]
+    start = lax.axis_index(AXES) * extent
+    rows = min(-(-extent // wide) + (1 if extent % wide else 0), left.shape[1])
+    top = jnp.minimum(start // wide, left.shape[1] - rows)
+    part = lax.dynamic_slice_in_dim(left, top, rows, 1)
+    whole = dot(part, right, (0, 0)).reshape(-1)
+    if rows * wide == extent:
+        return whole
+    return lax.dynamic_slice_in_dim(whole, start - top * wide, extent, 0)
 
 
 def solution(mesh):

time: 167 us -> 165 us (0.988)
  Pallas kernels: 122 us -> 116 us
  other arithmetic: 2.72 us -> 5.56 us
    pallas_call x1, Pallas kernels: 43.5 us -> 37.7 us  [scatter_sum(): pl.pallas_call(partial(scatter_kernel, grid, chunks, len(arrays)), out_sh...]
    another operation x1 -> x2, local copies, waits for them, and re-layouts: 4.5 us -> 1.35 us  [pack(): parts.append(piece.reshape(lead + (rows, LANES)))]
    slice x1 -> x2, local copies, waits for them, and re-layouts: 1.23 us -> 4.35 us  [unpack(): attn_flat[:qkv_size].reshape(model_width, 3 * model_width)]
    concatenate x1 -> x0, local copies, waits for them, and re-layouts: 2.52 us -> none  [pack(): return jnp.concatenate(parts, axis=-2)]
    slice x1 -> x2, local copies, waits for them, and re-layouts: 0.98 us -> 3.09 us  [unpack(): attn_flat[qkv_size:].reshape(model_width, model_width)]
    unnamed x13 -> x32, local copies, waits for them, and re-layouts: 7.52 us -> 7.26 us
where the time goes in v3:
time: 165 us
  Pallas kernels  116 us (70%)
  local copies, waits for them, and re-layouts  41.2 us (25%)
  other arithmetic  5.56 us (3%)
    pallas_call x1, Pallas kernels, gather_all(): pl.pallas_call(partial(gather_kernel, grid, chunks, len(arrays)), out_sha...  42.8 us
    pallas_call x1, Pallas kernels, scatter_sum(): pl.pallas_call(partial(scatter_kernel, grid, chunks, len(arrays)), out_sh...  37.7 us
    pallas_call x1, Pallas kernels, run_block(): pl.pallas_call(block_kernel, out_shape=[jax.ShapeDtypeStruct(shape, kind)...  35.5 us
    unnamed x32, local copies, waits for them, and re-layouts  7.26 us
    concatenate x2, local copies, waits for them, and re-layouts, local(): jnp.concatenate([g_one.reshape(-1), g_two.reshape(-1)])  4.42 us
    slice x2, local copies, waits for them, and re-layouts, unpack(): attn_flat[:qkv_size].reshape(model_width, 3 * model_width)  4.35 us
    reshape x1, local copies, waits for them, and re-layouts, unpack(): mlp_flat[:fc1_size].reshape(model_width, hidden_units)  3.47 us

profile of v3, /device:TPU:0, one launch (start us, length us, event | category | flops | bytes accessed | tf_op | source)
XLA Modules:
  0.0 164.5 jit_solution(5756109364487915139)
XLA Ops:
  1.3 0.9 copy-done.6
  3.8 42.8 %shard_map.135 = (bf16[2,2,4,2,216,128]{5,4,3,2,1,0:T(8,128)(2,1)S(1)}, bf16[2,2,4,2,144,128]{5,4,3,2,1,0:T(8,128)(2,1)S(1)}, bf16[2,2,4,2,288,128]{5,4,3,2,1,0:...) custom-call(bf16[216,128]{1,0:T(8,128)(2,1)S(1)} %bitcast.33, bf16[144,128]{1,0:T(8,128)(2,1)S(1)} %bitcast.34, ...), custom_call_target="tpu_custom_call" | custom-call | tf_op jit(solution)/shard_map/pallas_call | solution.py:243
  46.6 1.6 fusion.3
  48.1 3.5 %reshape.98.w_one = bf16[384,1536]{1,0:T(8,128)(2,1)} reshape(bf16[1,2,4,2,288,128]{5,4,3,2,1,0:T(8,128)(2,1)} %get-tuple-element.44) | data formatting | bytes 2359296 | tf_op jit(solution)/shard_map/reshape | solution.py:56
  51.6 3.1 %reshape.99.w_two = bf16[1536,384]{1,0:T(8,128)(2,1)} reshape(bf16[1,2,4,2,288,128]{5,4,3,2,1,0:T(8,128)(2,1)} %get-tuple-element.43) | data formatting | bytes 2359296 | tf_op jit(solution)/shard_map/reshape | solution.py:57
  54.7 2.2 %slice.32 = bf16[512,1152]{1,0:T(8,128)(2,1)} reshape(bf16[2,2,4,2,144,128]{5,4,3,2,1,0:T(8,128)(2,1)S(1)} %get-tuple-element.26) | data formatting | bytes 2359296 | tf_op jit(solution)/shard_map/slice | solution.py:54
  56.9 2.2 %slice.42.w_qkv = bf16[384,1152]{1,0:T(8,128)(2,1)} slice(bf16[512,1152]{1,0:T(8,128)(2,1)} %slice.32), slice={[0:384], [0:1152]} | slice | bytes 1769472 | tf_op jit(solution)/shard_map/slice | solution.py:54
  59.0 1.4 slice.34
  60.4 1.7 %slice.43.w_proj = bf16[384,384]{1,0:T(8,128)(2,1)} slice(bf16[1536,384]{1,0:T(8,128)(2,1)} %slice.34), slice={[1152:1536], [0:384]} | slice | bytes 589824 | tf_op jit(solution)/shard_map/slice | solution.py:55
  62.1 3.0 %reshape_reshape_reshape.3.w_ada = bf16[384,2304]{1,0:T(8,128)(2,1)} reshape(bf16[2,2,4,2,216,128]{5,4,3,2,1,0:T(8,128)(2,1)S(1)} %get-tuple-element.25) | data formatting | bytes 3538944 | tf_op jit(solution)/shard_map/reshape;reshape;reshape | solution.py:53
  66.5 35.5 %shard_map.136 = (f32[4,128,384]{2,1,0:T(8,128)}, f32[4,128,384]{2,1,0:T(8,128)}, f32[4,384]{1,0:T(4,128)}, bf16[4,384]{1,0:T(4,128)(2,1)}, bf16[4,2304]{1,0:T(4...) custom-call(s32[1]{0:T(128)S(6)} %copy.21.count_ref, ...), custom_call_target="tpu_custom_call" | custom-call | tf_op jit(solution)/shard_map/pallas_call | solution.py:619
  102.0 3.0 %concatenate.16 = bf16[1,2,4,2,288,128]{5,4,3,2,1,0:T(8,128)(2,1)S(1)} reshape(bf16[384,1536]{1,0:T(8,128)(2,1)} %get-tuple-element.36) | data formatting | bytes 2359296 | tf_op jit(solution)/shard_map/concatenate | solution.py:654
  105.1 1.4 concatenate.17
  106.5 1.5 pad_maximum_fusion.refs_1_
  108.0 2.8 %reshape.101 = bf16[442368]{0:T(1024)(128)(2,1)} reshape(bf16[384,1152]{1,0:T(8,128)(2,1)} %get-tuple-element.34) | data formatting | bytes 1769472 | tf_op jit(solution)/shard_map/reshape | solution.py:653
  110.8 0.9 reshape.102
  111.6 1.3 pad_maximum_fusion.1
  113.0 1.3 reshape_reshape.15
  114.3 1.3 pad_maximum_fusion.2.note_ref
  115.7 1.4 convert_reduce_fusion
  117.1 0.8 reshape_reshape.18
  120.0 37.7 %shard_map.137 = (bf16[2,2,4,2,84,128]{5,4,3,2,1,0:T(8,128)(2,1)S(1)}, f32[144,128]{1,0:T(8,128)S(1)}, f32[288,128]{1,0:T(8,128)S(1)}, f32[2,128]{1,0:T(2,128)S(1)}) custom-call(bf16[84,128]{1,0:T(8,128)(2,1)S(1)} %copy-done.3, bf16[2,2,4,2,144,128]{5,4,3,2,1,0:T(8,128)(2,1)S(1)} %bitcast.27, bf16[2,2,4,2,288,128]{5,4,3,2,1,0:T(8,128)(2,1)S(1)} %pad_maximum_fusion.refs_1_, ...), custom_call_target="tpu_custom_call" | custom-call | tf_op jit(solution)/shard_map/pallas_call | solution.py:374
  159.0 0.9 copy-done
  160.6 0.9 slice.45
  (41 shorter events, 10.0 us)
Async XLA Ops:
  1.3 0.9 copy-start.6
  2.2 0.8 copy-start.7
  3.0 0.8 copy-start.8
  102.0 3.0 %copy-start.11 = (bf16[1536,384]{1,0:T(8,128)(2,1)S(1)}, bf16[1536,384]{1,0:T(8,128)(2,1)}, u32[]{:S(2)}) copy-start(bf16[1536,384]{1,0:T(8,128)(2,1)} %get-tuple-element.37) | copy-start | bytes 3538948
  108.0 2.8 %copy-start.12 = (bf16[384,384]{1,0:T(8,128)(2,1)S(1)}, bf16[384,384]{1,0:T(8,128)(2,1)}, u32[]{:S(2)}) copy-start(bf16[384,384]{1,0:T(8,128)(2,1)} %get-tuple-element.35) | copy-start | bytes 884740
  111.6 2.7 %copy-start.13 = (bf16[4,384]{1,0:T(4,128)(2,1)S(1)}, bf16[4,384]{1,0:T(4,128)(2,1)}, u32[]{:S(2)}) copy-start(bf16[4,384]{1,0:T(4,128)(2,1)} %get-tuple-element.33) | copy-start | bytes 9220
  119.2 0.7 copy-start.3
  157.7 0.7 copy-start.1
  158.3 0.6 copy-start.4
  159.0 0.9 copy-start
  159.0 0.9 copy-start.9
  159.9 2.7 %copy-start.5 = (f32[144,128]{1,0:T(8,128)S(1)}, f32[144,128]{1,0:T(8,128)}, u32[]{:S(2)}) copy-start(f32[144,128]{1,0:T(8,128)} %copy-done.4) | copy-start | bytes 221188
  159.9 3.4 %copy-start.2 = (f32[288,128]{1,0:T(8,128)S(1)}, f32[288,128]{1,0:T(8,128)}, u32[]{:S(2)}) copy-start(f32[288,128]{1,0:T(8,128)} %copy-done.1) | copy-start | bytes 442372
  160.6 3.3 %copy-start.10 = (f32[2,128]{1,0:T(2,128)S(1)}, f32[2,128]{1,0:T(2,128)}, u32[]{:S(2)}) copy-start(f32[2,128]{1,0:T(2,128)} %copy-done.9) | copy-start | bytes 3076

commit v4 on v3

--- a/solution.py
+++ b/solution.py
@@ -44,30 +44,6 @@
 def silu_slope(values):
     sigma = jax.nn.sigmoid(values)
     return sigma * (1.0 + values * (1.0 - sigma))
-
-
-def unpack(ada_flat, attn_flat, mlp_flat, bias_flat, model_width, hidden_units):
-    qkv_size = 3 * model_width * model_width
-    fc1_size = model_width * hidden_units
-    pieces = [
-        ada_flat.reshape(model_width, 6 * model_width),
-        attn_flat[:qkv_size].reshape(model_width, 3 * model_width),
-        attn_flat[qkv_size:].reshape(model_width, model_width),
-        mlp_flat[:fc1_size].reshape(model_width, hidden_units),
-        mlp_flat[fc1_size:].reshape(hidden_units, model_width),
-    ]
-    offset = 0
-    for extent_now in [
-        6 * model_width,
-        model_width,
-        model_width,
-        model_width,
-        hidden_units,
-        model_width,
-    ]:
-        pieces.append(bias_flat[offset : offset + extent_now])
-        offset = offset + extent_now
-    return tuple(pieces)
 
 
 LANES = 128
@@ -256,9 +232,10 @@
     )(*arrays)
 
 
-def scatter_kernel(grid, chunks, arrays, note_ref, *refs):
+def scatter_kernel(grid, chunks, arrays, extra, *refs):
+    note_refs, refs = refs[:extra], refs[extra:]
     g_refs, refs = refs[:arrays], refs[arrays:]
-    note_out, refs = refs[0], refs[1:]
+    note_outs, refs = refs[:extra], refs[extra:]
     out_refs, refs = refs[:arrays], refs[arrays:]
     pair_bufs, refs = refs[:arrays], refs[arrays:]
     accs, refs = refs[:arrays], refs[arrays:]
@@ -269,10 +246,17 @@
     here, push = mover.here, mover.push
     hi, lo, z, c = here
     grid.barrier(here)
-    own = pltpu.make_async_copy(note_ref, note_out.at[hi, lo, z, c], own_sem)
-    own.start()
-    note = Spread(mover, note_ref, note_out, pl.ds(0, note_ref.shape[0]), True)
-    note.begin()
+    owns = [
+        pltpu.make_async_copy(note_refs[n], note_outs[n].at[hi, lo, z, c], own_sem.at[n])
+        for n in range(extra)
+    ]
+    notes = [
+        Spread(mover, note_refs[n], note_outs[n], pl.ds(0, note_refs[n].shape[0]), n % 2 == 0)
+        for n in range(extra)
+    ]
+    for own, note in zip(owns, notes):
+        own.start()
+        note.begin()
 
     def steps(axis):
         return [(s - 1, grid.peer(here, axis, s)) for s in range(1, grid.sizes[axis])]
@@ -297,8 +281,9 @@
         swaps.append(
             [push(g_ref.at[:, :, :, spot[3], rows], pair_buf.at[:, :, :, rows], spot) for _, spot in steps(3)]
         )
-    own.wait()
-    note.first()
+    for own, note in zip(owns, notes):
+        own.wait()
+        note.first()
     for k, (n, start, size) in enumerate(chunks):
         rows = pl.ds(start, size)
         g_ref, pair_buf, acc, buf_one = g_refs[n], pair_bufs[n], accs[n], one_bufs[n]
@@ -315,7 +300,8 @@
             ones.append(
                 [push(acc.at[:, spot[1], :, rows], buf_one.at[s, 0:high, :, rows], spot) for s, spot in steps(1)]
             )
-    note.second()
+    for note in notes:
+        note.second()
     for k, (n, start, size) in enumerate(chunks):
         rows = pl.ds(start, size)
         acc, buf_one, buf_two = accs[n], one_bufs[n], two_bufs[n]
@@ -334,7 +320,8 @@
             twos.append(
                 [push(acc.at[spot[0], lo, :, rows], buf_two.at[s, :, rows], spot) for s, spot in steps(0)]
             )
-    note.third()
+    for note in notes:
+        note.third()
     for k, (n, start, size) in enumerate(chunks):
         rows = pl.ds(start, size)
         acc, buf_two, buf_z = accs[n], two_bufs[n], z_bufs[n]
@@ -355,14 +342,15 @@
         for s in range(depth - 1):
             total = total + buf_z[s, rows].astype(jnp.float32)
         out_refs[n][rows, :] = total
-    note.end()
+    for note in notes:
+        note.end()
     mover.drain()
 
 
-def scatter_sum(grid, arrays, note):
+def scatter_sum(grid, arrays, notes):
     high, low, depth, pair = grid.sizes
     chunks = chunk_rows(arrays)
-    copies = len(chunks) * (high + low + depth + pair - 4) + Spread.copies(grid)
+    copies = len(chunks) * (high + low + depth + pair - 4) + Spread.copies(grid) * len(notes)
     kind = arrays[0].dtype
     tails = [array.shape[-2:] for array in arrays]
     side = max(high, low)
@@ -372,17 +360,17 @@
     ]
     vmem = pl.BlockSpec(memory_space=pltpu.VMEM)
     return pl.pallas_call(
-        partial(scatter_kernel, grid, chunks, len(arrays)),
-        out_shape=[jax.ShapeDtypeStruct(grid.sizes + note.shape, note.dtype)]
+        partial(scatter_kernel, grid, chunks, len(arrays), len(notes)),
+        out_shape=[jax.ShapeDtypeStruct(grid.sizes + note.shape, note.dtype) for note in notes]
         + [jax.ShapeDtypeStruct(tail, jnp.float32) for tail in tails],
-        in_specs=[vmem] * (1 + len(arrays)),
-        out_specs=[vmem] * (1 + len(arrays)),
+        in_specs=[vmem] * (len(notes) + len(arrays)),
+        out_specs=[vmem] * (len(notes) + len(arrays)),
         scratch_shapes=[pltpu.VMEM(shape + tail, kind) for shape in shapes for tail in tails]
-        + [pltpu.SemaphoreType.DMA((copies,)), pltpu.SemaphoreType.DMA((copies,)), pltpu.SemaphoreType.DMA],
+        + [pltpu.SemaphoreType.DMA((copies,)), pltpu.SemaphoreType.DMA((copies,)), pltpu.SemaphoreType.DMA((len(notes),))],
         compiler_params=pltpu.CompilerParams(
             collective_id=1, has_side_effects=True, vmem_limit_bytes=48 * 1024 * 1024
         ),
-    )(note, *arrays)
+    )(*notes, *arrays)
 
 
 def padded_rows(extent):
@@ -410,8 +398,9 @@
 
 
 def block_kernel(
-    count_ref, x_ref, cond_ref, cot_ref, w_ada, w_qkv, w_proj, w_one, w_two, bias_ref,
-    out_ref, gx_ref, gcond_ref, act_ref, dmod_ref, g_qkv, g_proj, g_one, g_two, gbias_ref,
+    count_ref, x_ref, cond_ref, cot_ref, w_ada, attn_ref, mlp_ref, bias_ref,
+    out_ref, gx_ref, gcond_ref, act_ref, dmod_ref, g_attn, g_mlp, gbias_ref,
+    line, w_qkv, w_proj, w_one, w_two, g_qkv, g_proj, g_one, g_two,
     mod, norm_one, inv_one, h_one, qkv, probs, mixed, branch, norm_two, inv_two, h_two,
     pre, act, mlp, wide, back, dx, small, dqkv, dmod,
 ):
@@ -445,6 +434,37 @@
     def column_sum(values):
         return jnp.sum(values, axis=0, keepdims=True)
 
+    def load_matrix(flat_ref, top, matrix):
+        height, across = matrix.shape[0], matrix.shape[1] // LANES
+        total = height * across
+
+        def widen(t, _):
+            at = pl.multiple_of(t * LANES, LANES)
+            line[pl.ds(at, LANES), :] = flat_ref[pl.ds(top + at, LANES), :].astype(f32)
+            return 0
+
+        lax.fori_loop(0, total // LANES, widen, 0)
+        for j in range(across):
+            matrix[:, j * LANES : (j + 1) * LANES] = line[pl.ds(j, height, stride=across), :].astype(b16)
+
+    def store_matrix(matrix, flat_ref, top):
+        height, across = matrix.shape[0], matrix.shape[1] // LANES
+        total = height * across
+        for j in range(across):
+            line[pl.ds(j, height, stride=across), :] = matrix[:, j * LANES : (j + 1) * LANES].astype(f32)
+
+        def narrow(t, _):
+            at = pl.multiple_of(t * LANES, LANES)
+            flat_ref[pl.ds(top + at, LANES), :] = line[pl.ds(at, LANES), :].astype(b16)
+            return 0
+
+        lax.fori_loop(0, total // LANES, narrow, 0)
+
+    proj_top, two_top = 3 * width * width // LANES, width * hidden // LANES
+    load_matrix(attn_ref, 0, w_qkv)
+    load_matrix(attn_ref, proj_top, w_proj)
+    load_matrix(mlp_ref, 0, w_one)
+    load_matrix(mlp_ref, two_top, w_two)
     cond = cond_ref[...]
     cond_act = (cond * jax.nn.sigmoid(cond)).astype(b16)
     mod[...] = dot(cond_act, w_ada[...]) + bias_ref[:, : 6 * width]
@@ -591,6 +611,10 @@
     slot_loop(attn_back)
     gbias_ref[:, : 6 * width] = column_sum(dmod[...])
     grad_mod = dmod[...].astype(b16)
+    store_matrix(g_qkv, g_attn, 0)
+    store_matrix(g_proj, g_attn, proj_top)
+    store_matrix(g_one, g_mlp, 0)
+    store_matrix(g_two, g_mlp, two_top)
     act_ref[...] = cond_act
     dmod_ref[...] = grad_mod
     gcond_ref[...] = dot(grad_mod, w_ada[...], (1, 1)) * silu_slope(cond)
@@ -598,16 +622,19 @@
 
 def run_block(counts, latents, conditioning, cotangent, weights, biases):
     slots, length, width = latents.shape
-    w_ada, w_qkv, w_proj, w_one, w_two = weights
-    hidden = w_one.shape[1]
+    w_ada, attn, mlp = weights
+    hidden = mlp.size // (2 * width)
     rows = slots * length
     f32, b16 = jnp.float32, jnp.bfloat16
     outs = [
         (latents.shape, f32), (latents.shape, f32), (conditioning.shape, f32),
-        (conditioning.shape, b16), ((slots, 6 * width), b16), (w_qkv.shape, b16), (w_proj.shape, b16), (w_one.shape, b16),
-        (w_two.shape, b16), (biases.shape, f32),
+        (conditioning.shape, b16), ((slots, 6 * width), b16),
+        (attn.shape, b16), (mlp.shape, b16), (biases.shape, f32),
     ]
-    scratch = [
+    matrices = [(width, 3 * width), (width, width), (width, hidden), (hidden, width)]
+    scratch = [((max(h * w for h, w in matrices) // LANES, LANES), f32)]
+    scratch += [(shape, b16) for shape in matrices + matrices]
+    scratch += [
         ((slots, 6 * width), f32), ((rows, width), f32), ((rows, 1), f32), ((rows, width), b16),
         ((rows, 3 * width), b16), ((slots, HEADS, length, length), f32), ((rows, width), b16),
         ((rows, width), f32), ((rows, width), f32), ((rows, 1), f32), ((rows, width), b16),
@@ -619,7 +646,7 @@
     return pl.pallas_call(
         block_kernel,
         out_shape=[jax.ShapeDtypeStruct(shape, kind) for shape, kind in outs],
-        in_specs=[pl.BlockSpec(memory_space=pltpu.SMEM)] + [vmem] * 9,
+        in_specs=[pl.BlockSpec(memory_space=pltpu.SMEM)] + [vmem] * 7,
         out_specs=[vmem] * len(outs),
         scratch_shapes=[pltpu.VMEM(shape, kind) for shape, kind in scratch],
         compiler_params=pltpu.CompilerParams(vmem_limit_bytes=60 * 1024 * 1024),
@@ -632,36 +659,31 @@
     model_width = latents.shape[-1]
     slots = latents.shape[0]
     shards = (ada_weights, attn_weights, mlp_weights, flat_biases)
-    flats = [
-        whole.reshape(grid.count, -1)[:, : shard.shape[0]].reshape(-1)
-        for whole, shard in zip(gather_all(grid, [pack([shard], ()) for shard in shards]), shards)
-    ]
-    weights = unpack(flats[0], flats[1], flats[2], flats[3], model_width, FF)[:5]
-    biases = flats[3].astype(jnp.float32)[None]
-    output, grad_latents, grad_conditioning, cond_act, grad_mod, g_qkv, g_proj, g_one, g_two, g_bias = (
+    whole_ada, whole_attn, whole_mlp, whole_bias = gather_all(
+        grid, [pack([shard], ()) for shard in shards]
+    )
+    bias_flat = whole_bias.reshape(grid.count, -1)[:, : flat_biases.shape[0]].reshape(-1)
+    weights = (
+        whole_ada.reshape(model_width, 6 * model_width),
+        whole_attn.reshape(-1, LANES),
+        whole_mlp.reshape(-1, LANES),
+    )
+    biases = bias_flat.astype(jnp.float32)[None]
+    output, grad_latents, grad_conditioning, cond_act, grad_mod, g_attn, g_mlp, g_bias = (
         run_block(counts, latents, conditioning, cotangent, weights, biases)
     )
 
-    def lines(flat, extent):
-        rows = padded_rows(extent)
-        flat = flat.reshape(grid.count, extent)
-        if rows * LANES != extent:
-            flat = jnp.pad(flat, ((0, 0), (0, rows * LANES - extent)))
-        return flat.reshape(grid.sizes + (rows, LANES))
-
-    flat_grads = [
-        jnp.concatenate([g_qkv.reshape(-1), g_proj.reshape(-1)]),
-        jnp.concatenate([g_one.reshape(-1), g_two.reshape(-1)]),
-        g_bias.astype(jnp.bfloat16).reshape(-1),
-    ]
-    note = pack([grad_mod.reshape(-1), cond_act.reshape(-1)], ())
-    notes, *sums = scatter_sum(
-        grid, [lines(flat, shard.shape[0]) for flat, shard in zip(flat_grads, shards[1:])], note
+    gap = padded_rows(flat_biases.shape[0]) * LANES - flat_biases.shape[0]
+    bias_lines = jnp.pad(
+        g_bias.astype(jnp.bfloat16).reshape(grid.count, -1), ((0, 0), (0, gap))
     )
-    notes = notes.reshape((grid.count,) + note.shape)
-    mod_rows, act_rows = grad_mod.size // LANES, cond_act.size // LANES
-    all_mod = notes[:, :mod_rows].reshape(grid.count * slots, 6 * model_width)
-    all_act = notes[:, mod_rows : mod_rows + act_rows].reshape(grid.count * slots, model_width)
+    all_mod, all_act, *sums = scatter_sum(
+        grid,
+        [flat.reshape(grid.sizes + (-1, LANES)) for flat in (g_attn, g_mlp, bias_lines)],
+        [grad_mod, cond_act],
+    )
+    all_mod = all_mod.reshape(grid.count * slots, -1)
+    all_act = all_act.reshape(grid.count * slots, -1)
     grads = [own_rows(all_act, all_mod, ada_weights.shape[0])]
     grads += [total.reshape(-1)[: shard.shape[0]] for total, shard in zip(sums, shards[1:])]
     return (output, grad_latents, grad_conditioning) + tuple(grads)

time: 165 us -> 139 us (0.84)
  local copies, waits for them, and re-layouts: 41.2 us -> 16.4 us
  other arithmetic: 5.56 us -> 0.8 us
  Pallas kernels: 116 us -> 119 us
    slice x7 -> x0, local copies, waits for them, and re-layouts: 9.97 us -> none  [the longest x2 4.35 us: unpack(): attn_flat[:qkv_size].reshape(model_width, 3 * model_width)]
    reshape x7 -> x5, local copies, waits for them, and re-layouts: 11.7 us -> 3.27 us  [the longest x1 2.98 us: local(): whole_ada.reshape(model_width, 6 * model_width)]
    another operation x4 -> x0, local copies, waits for them, and re-layouts: 5.15 us -> none  [the longest x1 2.99 us: unpack(): ada_flat.reshape(model_width, 6 * model_width)]
    concatenate x2 -> x0, local copies, waits for them, and re-layouts: 4.42 us -> none  [local(): jnp.concatenate([g_one.reshape(-1), g_two.reshape(-1)])]
    concatenate x3 -> x0, other arithmetic: 4.16 us -> none  [the longest x1 1.49 us: local(): jnp.concatenate([g_one.reshape(-1), g_two.reshape(-1)])]
    unnamed x32 -> x22, local copies, waits for them, and re-layouts: 7.26 us -> 11.1 us
    pallas_call x1, Pallas kernels: 35.5 us -> 38.6 us  [run_block(): pl.pallas_call(block_kernel, out_shape=[jax.ShapeDtypeStruct(shape, kind)...]
where the time goes in v4:
time: 139 us; the launch traced here: 138 us
  Pallas kernels  119 us (86%)
  local copies, waits for them, and re-layouts  16.4 us (12%)
    pallas_call x1, Pallas kernels, gather_all(): pl.pallas_call(partial(gather_kernel, grid, chunks, len(arrays)), out_sha...  42.8 us
    pallas_call x1, Pallas kernels, run_block(): pl.pallas_call(block_kernel, out_shape=[jax.ShapeDtypeStruct(shape, kind)...  38.6 us
    pallas_call x1, Pallas kernels, scatter_sum(): pl.pallas_call(partial(scatter_kernel, grid, chunks, len(arrays), len(not...  37.8 us
    unnamed x22, local copies, waits for them, and re-layouts  11.1 us
    reshape x1, local copies, waits for them, and re-layouts, local(): whole_ada.reshape(model_width, 6 * model_width)  2.98 us

profile of v4, /device:TPU:0, one launch (start us, length us, event | category | flops | bytes accessed | tf_op | source)
XLA Modules:
  0.0 138.2 jit_solution(12628084949511569717)
XLA Ops:
  0.6 0.7 pad_bitcast_fusion.refs_3_
  1.3 0.9 copy-done.4
  2.2 0.8 copy-done.5
  3.0 0.8 copy-done.6
  3.8 42.8 %shard_map.135 = (bf16[2,2,4,2,216,128]{5,4,3,2,1,0:T(8,128)(2,1)S(1)}, bf16[2,2,4,2,144,128]{5,4,3,2,1,0:T(8,128)(2,1)S(1)}, bf16[2,2,4,2,288,128]{5,4,3,2,1,0:...) custom-call(bf16[216,128]{1,0:T(8,128)(2,1)S(1)} %bitcast.28, bf16[144,128]{1,0:T(8,128)(2,1)S(1)} %bitcast.29, ...), custom_call_target="tpu_custom_call" | custom-call | tf_op jit(solution)/shard_map/pallas_call | solution.py:219
  46.6 0.0 copy-start.1
  46.6 1.4 %copy-done.1 = bf16[2,2,4,2,288,128]{5,4,3,2,1,0:T(8,128)(2,1)} copy-done((bf16[2,2,4,2,288,128]{5,4,3,2,1,0:T(8,128)(2,1)}, bf16[2,2,4,2,288,128]{5,4,3,2,1,0:T(8,128)(2,1)S(1)}, u32[]{:S(2)}) %copy-start.1) | copy-done | bytes 2359320
  48.0 1.0 copy-done.3
  49.0 3.0 %reshape.85.w_ada = bf16[384,2304]{1,0:T(8,128)(2,1)} reshape(bf16[2,2,4,2,216,128]{5,4,3,2,1,0:T(8,128)(2,1)S(1)} %get-tuple-element.24) | data formatting | bytes 3538944 | tf_op jit(solution)/shard_map/reshape | solution.py:667
  52.0 0.7 reshape.99.bias_ref
  53.4 38.6 %shard_map.136 = (f32[4,128,384]{2,1,0:T(8,128)}, f32[4,128,384]{2,1,0:T(8,128)}, f32[4,384]{1,0:T(4,128)}, bf16[4,384]{1,0:T(4,128)(2,1)}, bf16[4,2304]{1,0:T(4...) custom-call(s32[1]{0:T(128)S(6)} %copy.21.count_ref, f32[4,128,384]{2,1,0:T(8,128)} %x_ref.1, ...), custom_call_target="tpu_custom_call" | custom-call | tf_op jit(solution)/shard_map/pallas_call | solution.py:646
  92.0 0.8 convert_reduce_fusion
  92.8 0.1 reshape.91
  92.9 1.7 %copy-done = bf16[9216,128]{1,0:T(8,128)(2,1)S(1)} copy-done((bf16[9216,128]{1,0:T(8,128)(2,1)S(1)}, bf16[9216,128]{1,0:T(8,128)(2,1)}, u32[]{:S(2)}) %copy-start) | copy-done | bytes 2359320
  94.6 1.3 copy-done.2
  95.9 0.7 copy-done.7
  96.6 0.7 copy-done.8
  97.3 37.8 %shard_map.137 = (bf16[2,2,4,2,4,2304]{5,4,3,2,1,0:T(4,128)(2,1)S(1)}, bf16[2,2,4,2,4,384]{5,4,3,2,1,0:T(4,128)(2,1)S(1)}, f32[144,128]{1,0:T(8,128)S(1)}, f32[288,128]{1,0:T(8,128)S(1)}, f32[2,128]{1,0:T(2,128)S(1)}) custom-call(bf16[4,2304]{1,0:T(4,128)(2,1)S(1)} %copy-done.7, bf16[4,384]{1,0:T(4,128)(2,1)S(1)} %copy-done.8, ...), custom_call_target="tpu_custom_call" | custom-call | tf_op jit(solution)/shard_map/pallas_call | solution.py:362
  135.1 0.1 reshape.94
  135.3 0.3 fusion
  135.6 0.7 reshape.95
  136.3 0.6 copy.22
  136.9 0.7 copy.23
  137.6 0.6 copy.24
  (13 shorter events, 0.1 us)
Async XLA Ops:
  1.3 0.9 copy-start.4
  2.2 0.8 copy-start.5
  3.0 0.8 copy-start.6
  46.6 1.4 %copy-start.1 = (bf16[2,2,4,2,288,128]{5,4,3,2,1,0:T(8,128)(2,1)}, bf16[2,2,4,2,288,128]{5,4,3,2,1,0:T(8,128)(2,1)S(1)}, u32[]{:S(2)}) copy-start(bf16[2,2,4,2,288,128]{5,4,3,2,1,0:T(8,128)(2,1)S(1)} %get-tuple-element.26) | copy-start | bytes 7077892
  48.0 1.0 copy-start.3
  92.9 1.7 %copy-start = (bf16[9216,128]{1,0:T(8,128)(2,1)S(1)}, bf16[9216,128]{1,0:T(8,128)(2,1)}, u32[]{:S(2)}) copy-start(bf16[9216,128]{1,0:T(8,128)(2,1)} %get-tuple-element.34) | copy-start | bytes 7077892
  94.6 1.3 copy-start.2
  95.9 0.7 copy-start.7
  96.6 0.7 copy-start.8
